TPU v7x, 32 devices: a whole 2x2x4 slice. The times are simulated.
32 devices in a mesh: noise: 8 (over z, x), qi: 2 (over core), kj: 2 (over y).
Axes of the slice: x: 2, y: 2, z: 4, core: 2. Of those that a mesh axis runs over, the one named last changes fastest.
Arguments:
- pair_rep: bfloat16 [128, 2, 64, 128], P('qi', None, 'kj'), may hold values from -6 to 6
- query_rows: bfloat16 [8, 128, 768], P('noise', 'qi'), may hold values from -10 to 10
- key_rows: bfloat16 [8, 2, 64, 768], P('noise', None, 'kj'), may hold values from -10 to 10
- value_rows: bfloat16 [8, 2, 64, 768], P('noise', None, 'kj'), may hold values from -6 to 6
- output_grad: bfloat16 [8, 128, 768], P('noise', 'qi'), may hold values from -24 to 24
- gain_first: float32 [128], replicated, may hold values from 0.5 to 1.5
- gate_weight: bfloat16 [128, 512], replicated, may hold values from -0.5 to 0.5
- up_weight: bfloat16 [128, 512], replicated, may hold values from -0.5 to 0.5
- down_weight: bfloat16 [512, 128], replicated, may hold values from -0.25 to 0.25
- gain_second: float32 [128], replicated, may hold values from 0.5 to 1.5
- head_weight: bfloat16 [128, 16], replicated, may hold values from -0.5 to 0.5
Outputs:
- query_grad: bfloat16 [8, 128, 768], P('noise', ('qi', 'kj'))
- key_grad: bfloat16 [8, 128, 768], P('noise', ('qi', 'kj'))
- value_grad: bfloat16 [8, 128, 768], P('noise', ('qi', 'kj'))
- pair_grad: bfloat16 [2, 8, 8, 2, 64, 128], P('qi', 'noise', None, None, 'kj')
- gate_grad: float32 [128, 512], replicated
- up_grad: float32 [128, 512], replicated
- down_grad: float32 [512, 128], replicated
- head_grad: float32 [128, 16], replicated
- first_grad: float32 [128], replicated
- second_grad: float32 [128], replicated
All inputs are finite; a program needn't handle non-finite values.
Results may differ from a plain program's by a relative error of at most 0.011.
Values may be sent and summed in bfloat16 or wider, within the bound.
A program may use at most 64 MiB of HBM per device.

v0:
```python
import functools

import jax
import jax.numpy as jnp
from jax import lax
from jax.experimental import pallas as pl
from jax.experimental.pallas import tpu as pltpu
from jax.sharding import PartitionSpec as P

HEADS = 16
HEAD_DIM = 48
ALIGN = 8
LANES = 128

epsilon = 1e-05
F32 = jnp.float32
BF16 = jnp.bfloat16
MESH = pl.DeviceIdType.MESH


def dot(left, right, left_dim, right_dim):
    return lax.dot_general(
        left, right, (((left_dim,), (right_dim,)), ((), ())), preferred_element_type=F32
    )


def normalize(values):
    center = values - jnp.mean(values, axis=1, keepdims=True)
    inverse = lax.rsqrt(jnp.mean(center * center, axis=1, keepdims=True) + epsilon)
    return center * inverse, inverse


def norm_backward(normed_grad, normed, inverse):
    first_mean = jnp.mean(normed_grad, axis=1, keepdims=True)
    second_mean = jnp.mean(normed_grad * normed, axis=1, keepdims=True)
    return inverse * (normed_grad - first_mean - normed * second_mean)


def kernel(
    sizes,
    pair_ref,
    q_ref,
    k_ref,
    v_ref,
    g_ref,
    gain_first_ref,
    gate_ref,
    up_ref,
    down_ref,
    gain_second_ref,
    head_ref,
    query_out,
    key_out,
    value_out,
    pair_out,
    weight_out,
    cells,
    pre_normed,
    pre_low,
    pre_low_t,
    gate_coef,
    up_coef,
    hidden,
    hidden_t,
    up_low,
    post_normed,
    post_low,
    inverses,
    bias_rows,
    bias_all,
    score,
    attend_grad,
    stats,
    grad_send,
    grad_recv,
    grad_sum,
    post_scaled,
    query_part,
    query_recv,
    kv_part,
    kv_recv,
    w_part,
    w_core,
    w_sum,
    w_recv,
    cell_sem,
    bias_send_sem,
    bias_recv_sem,
    stat_send_sem,
    stat_recv_sem,
    grad_send_sem,
    grad_recv_sem,
    query_send_sem,
    query_recv_sem,
    pair_sems,
    w_send_sem,
    w_recv_sem,
    all_send_sem,
    all_recv_sem,
    fwd_send_sem,
    fwd_recv_sem,
):
    n_noise, n_qi, n_kj, rows, keys, share, blocks = sizes
    group = n_noise * n_kj
    cell_count = share * keys
    chunk = min(256, cell_count)
    scale = HEAD_DIM ** (-0.5)
    noise = lax.axis_index("noise")
    qi = lax.axis_index("qi")
    kj = lax.axis_index("kj")
    me = noise * n_kj + kj
    sibling = {"qi": 1 - qi}
    channels = cells.shape[-1]
    width = q_ref.shape[-1]
    half = keys // n_qi
    q_half = rows // n_kj
    pack = max(1, LANES // keys)
    packed = HEADS // pack

    def members(p):
        return [p + j * packed for j in range(pack)]

    def remote(src, dst, send, recv, device):
        return pltpu.make_async_remote_copy(
            src_ref=src, dst_ref=dst, send_sem=send, recv_sem=recv, device_id=device, device_id_type=MESH
        )

    def of_group(index):
        return {"noise": index // n_kj, "kj": lax.rem(index, n_kj)}

    def each(count, body):
        def step(i, carry):
            body(i)
            return carry

        lax.fori_loop(1, count, step, 0)

    own = pltpu.make_async_copy(pair_ref.at[pl.ds(noise * share, share)], cells, cell_sem)
    own.start()

    barrier = pltpu.get_barrier_semaphore()

    def greet(i):
        pl.semaphore_signal(
            barrier, inc=1, device_id=of_group(lax.rem(me + i, group)), device_id_type=MESH
        )

    each(group, greet)
    pl.semaphore_signal(barrier, inc=1, device_id=sibling, device_id_type=MESH)
    own.wait()

    gain_first = gain_first_ref[...]
    gain_second = gain_second_ref[...]
    head_t = head_ref[...]
    flat_cells = cells[...].reshape(cell_count, channels)
    for start in range(0, cell_count, chunk):
        at = slice(start, start + chunk)
        inputs = flat_cells[at].astype(F32)
        normed, inverse = normalize(inputs)
        lowered = (normed * gain_first).astype(BF16)
        gate_pre = dot(lowered, gate_ref[...], 1, 0)
        up_pre = dot(lowered, up_ref[...], 1, 0)
        sigmoid = jax.nn.sigmoid(gate_pre)
        silu = gate_pre * sigmoid
        low_hidden = (silu * up_pre).astype(BF16)
        updated = inputs + dot(low_hidden, down_ref[...], 1, 0)
        after, after_inverse = normalize(updated)
        after_low = (after * gain_second).astype(BF16)
        pre_normed[at] = normed
        pre_low[at] = lowered
        gate_coef[at] = up_pre * sigmoid * (1.0 + gate_pre * (1.0 - sigmoid))
        up_coef[at] = silu
        hidden[at] = low_hidden
        post_normed[at] = after
        post_low[at] = after_low
        inverses[at, 0:1] = inverse
        inverses[at, 1:2] = after_inverse
    for i in range(share):
        bias_rows[i] = dot(head_t, post_low[i * keys : (i + 1) * keys], 1, 1)
    for p in range(packed):
        bias_all[noise, p] = jnp.concatenate([bias_rows[:, h, :] for h in members(p)], 1).astype(BF16)

    pl.semaphore_wait(barrier, group)

    def bias_copy(slot, peer):
        return remote(
            bias_all.at[slot], bias_all.at[slot], bias_send_sem.at[peer], bias_recv_sem.at[slot], {"noise": peer}
        )

    each(n_noise, lambda i: bias_copy(noise, lax.rem(noise + i, n_noise)).start())

    def head_of(ref, h):
        return ref[:, h * HEAD_DIM : (h + 1) * HEAD_DIM]

    for h in range(HEADS):
        score[h] = dot(head_of(q_ref, h), head_of(k_ref, h), 1, 1) * scale
        attend_grad[h] = dot(head_of(g_ref, h), head_of(v_ref, h), 1, 1)

    def bias_wait(i):
        peer = lax.rem(noise + n_noise - i, n_noise)
        bias_copy(peer, peer).wait_recv()

    hidden_t[...] = hidden[...].T
    pre_low_t[...] = pre_low[...].T
    w_part[...] = jnp.zeros(w_part.shape, BF16)
    each(n_noise, bias_wait)

    for h in range(HEADS):
        bias_at = slice(h // packed * keys, (h // packed + 1) * keys)
        full = score[h] + bias_all[:, h % packed].astype(F32).reshape(rows, pack * keys)[:, bias_at]
        largest = jnp.max(full, axis=1, keepdims=True)
        expo = jnp.exp(full - largest)
        score[h] = expo
        stats[kj, :, h : h + 1] = largest
        stats[kj, :, HEADS + h : HEADS + h + 1] = jnp.sum(expo, axis=1, keepdims=True)
        stats[kj, :, 2 * HEADS + h : 2 * HEADS + h + 1] = jnp.sum(
            expo * attend_grad[h], axis=1, keepdims=True
        )

    def stat_copy(slot, peer):
        return remote(
            stats.at[slot], stats.at[slot], stat_send_sem.at[peer], stat_recv_sem.at[slot], {"kj": peer}
        )

    each(n_kj, lambda i: stat_copy(kj, lax.rem(kj + i, n_kj)).start())

    def stat_wait(i):
        peer = lax.rem(kj + n_kj - i, n_kj)
        stat_copy(peer, peer).wait_recv()

    each(n_kj, stat_wait)

    parts = [stats[j] for j in range(n_kj)]
    row_max = parts[0][:, 0:HEADS]
    for part in parts[1:]:
        row_max = jnp.maximum(row_max, part[:, 0:HEADS])
    row_sum = jnp.zeros_like(row_max)
    row_dot = jnp.zeros_like(row_max)
    for part in parts:
        weight = jnp.exp(part[:, 0:HEADS] - row_max)
        row_sum += weight * part[:, HEADS : 2 * HEADS]
        row_dot += weight * part[:, 2 * HEADS : 3 * HEADS]
    factor = jnp.exp(stats[kj, :, 0:HEADS] - row_max) / row_sum
    delta = row_dot / row_sum
    for p in range(packed):
        pieces = []
        for h in members(p):
            attend = score[h] * factor[:, h : h + 1]
            score_grad = attend * (attend_grad[h] - delta[:, h : h + 1])
            score[h] = attend
            attend_grad[h] = score_grad
            pieces.append(score_grad)
        grad_send[:, p] = jnp.concatenate(pieces, 1).reshape(n_noise, share, pack * keys).astype(BF16)

    def grad_copy(slot, peer):
        return remote(
            grad_send.at[peer], grad_recv.at[slot], grad_send_sem.at[peer], grad_recv_sem.at[slot], {"noise": peer}
        )

    each(n_noise, lambda i: grad_copy(noise, lax.rem(noise + i, n_noise)).start())

    for h in range(HEADS):
        at = slice(h * HEAD_DIM, (h + 1) * HEAD_DIM)
        value_at = slice(width + h * HEAD_DIM, width + (h + 1) * HEAD_DIM)
        score_low = attend_grad[h].astype(BF16)
        attend_low = score[h].astype(BF16)
        query_part[:, :, at] = (
            (dot(score_low, head_of(k_ref, h), 1, 0) * scale).astype(BF16).reshape(n_kj, q_half, HEAD_DIM)
        )
        kv_part[:, :, at] = (
            (dot(score_low, head_of(q_ref, h), 0, 0) * scale).astype(BF16).reshape(n_qi, half, HEAD_DIM)
        )
        kv_part[:, :, value_at] = (
            dot(attend_low, head_of(g_ref, h), 0, 0).astype(BF16).reshape(n_qi, half, HEAD_DIM)
        )

    def query_copy(slot, peer):
        return remote(
            query_part.at[peer], query_recv.at[slot], query_send_sem.at[peer], query_recv_sem.at[slot], {"kj": peer}
        )

    each(n_kj, lambda i: query_copy(kj, lax.rem(kj + i, n_kj)).start())
    kv_copy = remote(kv_part.at[1 - qi], kv_recv, pair_sems.at[0], pair_sems.at[1], sibling)
    kv_copy.start()

    def grad_wait(i):
        peer = lax.rem(noise + n_noise - i, n_noise)
        grad_copy(peer, peer).wait_recv()

    grad_sum[...] = grad_send[noise].astype(F32)

    def grad_add(i):
        grad_wait(i)
        peer = lax.rem(noise + n_noise - i, n_noise)
        grad_sum[...] += grad_recv[peer].astype(F32)

    each(n_noise, grad_add)

    head_part = jnp.zeros((HEADS, channels), F32)
    for i in range(share):
        at = slice(i * keys, (i + 1) * keys)
        grad_row = grad_sum[:, i, :]
        grad_low = jnp.concatenate([grad_row[:, j * keys : (j + 1) * keys] for j in range(pack)], 0).astype(BF16)
        post_scaled[at] = dot(grad_low, head_t, 0, 0)
        head_part += dot(grad_low, post_low[at], 1, 0)
    hidden_count = gate_ref.shape[1]
    tiles = hidden_count // channels
    split = 3 * tiles // 2
    span = [group * part for part in blocks]
    base = [0, n_qi * span[0]]
    half_base = [0, span[0]]
    block_base = [0, blocks[0]]

    def put(t, value):
        first = t * channels if t < split else base[1] + (t - split) * channels
        w_part[first : first + channels] = value.astype(BF16)

    starts = range(0, cell_count, chunk)
    second_part = jnp.zeros((1, channels), F32)
    down_part = jnp.zeros((hidden_count, channels), F32)
    gate_part = jnp.zeros((channels, hidden_count), F32)
    for start in starts:
        at = slice(start, start + chunk)
        scaled = post_scaled[at]
        after = post_normed[at]
        second_part += jnp.sum(scaled * after, axis=0, keepdims=True)
        updated_grad = norm_backward(scaled * gain_second, after, inverses[at, 1:2])
        updated_low = updated_grad.astype(BF16)
        post_scaled[at] = updated_grad
        down_part += dot(hidden_t[:, at], updated_low, 1, 0)
        hidden_grad = dot(updated_low, down_ref[...], 1, 1)
        gate_low = (hidden_grad * gate_coef[at]).astype(BF16)
        up_low[at] = (hidden_grad * up_coef[at]).astype(BF16)
        gate_part += dot(pre_low_t[:, at], gate_low, 1, 0)
        hidden[at] = gate_low

    for t in range(tiles):
        at = slice(t * channels, (t + 1) * channels)
        put(t, down_part[at])
        put(tiles + t, gate_part[:, at])

    def half_rows(wave, core):
        return pl.ds(pl.multiple_of(base[wave] + core * span[wave], ALIGN), span[wave])

    def sum_rows(wave):
        return pl.ds(half_base[wave], span[wave])

    def core_copy(wave):
        return remote(
            w_part.at[half_rows(wave, 1 - qi)],
            w_core.at[sum_rows(wave)],
            pair_sems.at[2 + 2 * wave],
            pair_sems.at[3 + 2 * wave],
            sibling,
        )

    core_copy(0).start()

    first_part = jnp.zeros((1, channels), F32)
    up_part = jnp.zeros((channels, hidden_count), F32)
    for start in starts:
        at = slice(start, start + chunk)
        up_part += dot(pre_low_t[:, at], up_low[at], 1, 0)
        pre_scaled = dot(hidden[at], gate_ref[...], 1, 1) + dot(up_low[at], up_ref[...], 1, 1)
        first_part += jnp.sum(pre_scaled * pre_normed[at], axis=0, keepdims=True)
        post_normed[at] = pre_scaled
    for t in range(tiles):
        put(2 * tiles + t, up_part[:, t * channels : (t + 1) * channels])
    tail = base[1] + (3 * tiles - split) * channels
    w_part[tail : tail + HEADS] = head_part.astype(BF16)
    w_part[tail + HEADS : tail + 2 * HEADS] = jnp.concatenate(
        (
            jnp.broadcast_to(first_part, (HEADS // 2, channels)),
            jnp.broadcast_to(second_part, (HEADS // 2, channels)),
        ),
        0,
    ).astype(BF16)
    core_copy(1).start()

    def own_rows(wave, index):
        return pl.ds(pl.multiple_of(half_base[wave] + index * blocks[wave], ALIGN), blocks[wave])

    def w_copy(wave, slot, peer):
        return remote(
            w_sum.at[own_rows(wave, peer)],
            w_recv.at[slot, pl.ds(block_base[wave], blocks[wave])],
            w_send_sem.at[wave * group + peer],
            w_recv_sem.at[wave * group + slot],
            of_group(peer),
        )

    def out_rows(wave, core, index):
        return pl.ds(
            pl.multiple_of(base[wave] + core * span[wave] + index * blocks[wave], ALIGN), blocks[wave]
        )

    def all_copy(wave, slot, peer):
        at = out_rows(wave, qi, slot)
        return remote(
            weight_out.at[at],
            weight_out.at[at],
            all_send_sem.at[wave * group + peer],
            all_recv_sem.at[wave * group + slot],
            of_group(peer),
        )

    def fwd_copy(wave, core, slot):
        at = out_rows(wave, core, slot)
        return remote(
            weight_out.at[at],
            weight_out.at[at],
            fwd_send_sem.at[wave * group + slot],
            fwd_recv_sem.at[wave * group + slot],
            sibling,
        )

    for wave in range(2):
        core_copy(wave).wait_recv()
        w_sum[sum_rows(wave)] = (
            w_part[half_rows(wave, qi)].astype(F32) + w_core[sum_rows(wave)].astype(F32)
        ).astype(BF16)
        each(group, lambda i: w_copy(wave, me, lax.rem(me + i, group)).start())

    for start in starts:
        at = slice(start, start + chunk)
        inputs_grad = norm_backward(post_normed[at] * gain_first, pre_normed[at], inverses[at, 0:1])
        pair_out[at] = (post_scaled[at] + inputs_grad).astype(BF16)

    total = query_part[kj].astype(F32)

    def query_add(i, total):
        peer = lax.rem(kj + n_kj - i, n_kj)
        query_copy(peer, peer).wait_recv()
        return total + query_recv[peer].astype(F32)

    query_out[...] = lax.fori_loop(1, n_kj, query_add, total).astype(BF16)
    kv_copy.wait_recv()
    kv_total = kv_part[qi].astype(F32) + kv_recv[...].astype(F32)
    key_out[...] = kv_total[:, :width].astype(BF16)
    value_out[...] = kv_total[:, width:].astype(BF16)

    for wave in range(2):

        def w_add(i, total):
            peer = lax.rem(me + group - i, group)
            w_copy(wave, peer, peer).wait_recv()
            return total + w_recv[peer, pl.ds(block_base[wave], blocks[wave])].astype(F32)

        total = lax.fori_loop(1, group, w_add, w_sum[own_rows(wave, me)].astype(F32))
        weight_out[out_rows(wave, qi, me)] = (total * (1.0 / (rows * n_qi))).astype(BF16)
        each(group, lambda i: all_copy(wave, me, lax.rem(me + i, group)).start())
        fwd_copy(wave, qi, me).start()

    for wave in range(2):

        def forward(i):
            peer = lax.rem(me + group - i, group)
            all_copy(wave, peer, peer).wait_recv()
            fwd_copy(wave, qi, peer).start()

        each(group, forward)

    for wave in range(2):

        def fwd_wait(i, carry):
            fwd_copy(wave, 1 - qi, i).wait_recv()
            fwd_copy(wave, qi, i).wait_send()
            return carry

        lax.fori_loop(0, group, fwd_wait, 0)

        def drain(i):
            peer = lax.rem(me + i, group)
            w_copy(wave, me, peer).wait_send()
            all_copy(wave, me, peer).wait_send()

        each(group, drain)
        core_copy(wave).wait_send()

    def drain_noise(i):
        peer = lax.rem(noise + i, n_noise)
        bias_copy(noise, peer).wait_send()
        grad_copy(noise, peer).wait_send()

    each(n_noise, drain_noise)

    def drain_kj(i):
        peer = lax.rem(kj + i, n_kj)
        stat_copy(kj, peer).wait_send()
        query_copy(kj, peer).wait_send()

    each(n_kj, drain_kj)
    kv_copy.wait_send()


def finish(
    hidden_count,
    second_base,
    weight_ref,
    query_ref,
    key_ref,
    value_ref,
    pair_ref,
    query_out,
    key_out,
    value_out,
    pair_out,
    gate_out,
    up_out,
    down_out,
    head_out,
    first_out,
    second_out,
):
    query_out[...] = query_ref[...]
    key_out[...] = key_ref[...]
    value_out[...] = value_ref[...]
    pair_out[...] = pair_ref[...]
    channels = weight_ref.shape[1]
    tiles = hidden_count // channels
    split = 3 * tiles // 2

    def tile(t):
        first = t * channels if t < split else second_base + (t - split) * channels
        return weight_ref[first : first + channels].astype(F32)

    for t in range(tiles):
        at = slice(t * channels, (t + 1) * channels)
        down_out[at] = tile(t)
        gate_out[:, at] = tile(tiles + t)
        up_out[:, at] = tile(2 * tiles + t)
    tail = second_base + (3 * tiles - split) * channels
    head_out[...] = weight_ref[tail : tail + HEADS].astype(F32)
    small = weight_ref[tail + HEADS : tail + 2 * HEADS].astype(F32)
    first_out[...] = small[0:1]
    second_out[...] = small[HEADS // 2 : HEADS // 2 + 1]


def local(
    mesh_shape,
    pair_rep,
    query_rows,
    key_rows,
    value_rows,
    output_grad,
    gain_first,
    gate_weight,
    up_weight,
    down_weight,
    gain_second,
    head_weight,
):
    n_noise, n_qi, n_kj = mesh_shape
    rows, block_count, block_rows, channels = pair_rep.shape
    keys = block_count * block_rows
    width = query_rows.shape[2]
    share = rows // n_noise
    count = share * keys
    group = n_noise * n_kj
    hidden_count = gate_weight.shape[1]
    split = 3 * (hidden_count // channels) // 2 * channels
    wave_rows = (split, 3 * hidden_count - split + 2 * HEADS)
    blocks = tuple(-(-part // (n_qi * group * ALIGN)) * ALIGN for part in wave_rows)
    block = sum(blocks)
    second_base = n_qi * group * blocks[0]
    half = keys // n_qi
    q_half = rows // n_kj
    sizes = (n_noise, n_qi, n_kj, rows, keys, share, blocks)
    pack = max(1, LANES // keys)
    vmem = pl.BlockSpec(memory_space=pltpu.VMEM)
    dma = pltpu.SemaphoreType.DMA
    span = n_qi * group * block

    scratch = [
        pltpu.VMEM((share, block_count, block_rows, channels), BF16),
        pltpu.VMEM((count, channels), F32),
        pltpu.VMEM((count, channels), BF16),
        pltpu.VMEM((channels, count), BF16),
        pltpu.VMEM((count, hidden_count), F32),
        pltpu.VMEM((count, hidden_count), F32),
        pltpu.VMEM((count, hidden_count), BF16),
        pltpu.VMEM((hidden_count, count), BF16),
        pltpu.VMEM((count, hidden_count), BF16),
        pltpu.VMEM((count, channels), F32),
        pltpu.VMEM((count, channels), BF16),
        pltpu.VMEM((count, 128), F32),
        pltpu.VMEM((share, HEADS, keys), F32),
        pltpu.VMEM((n_noise, HEADS // pack, share, pack * keys), BF16),
        pltpu.VMEM((HEADS, rows, keys), F32),
        pltpu.VMEM((HEADS, rows, keys), F32),
        pltpu.VMEM((n_kj, rows, 128), F32),
        pltpu.VMEM((n_noise, HEADS // pack, share, pack * keys), BF16),
        pltpu.VMEM((n_noise, HEADS // pack, share, pack * keys), BF16),
        pltpu.VMEM((HEADS // pack, share, pack * keys), F32),
        pltpu.VMEM((count, channels), F32),
        pltpu.VMEM((n_kj, q_half, width), BF16),
        pltpu.VMEM((n_kj, q_half, width), BF16),
        pltpu.VMEM((n_qi, half, 2 * width), BF16),
        pltpu.VMEM((half, 2 * width), BF16),
        pltpu.VMEM((span, channels), BF16),
        pltpu.VMEM((group * block, channels), BF16),
        pltpu.VMEM((group * block, channels), BF16),
        pltpu.VMEM((group, block, channels), BF16),
        dma(()),
        dma((n_noise,)),
        dma((n_noise,)),
        dma((n_kj,)),
        dma((n_kj,)),
        dma((n_noise,)),
        dma((n_noise,)),
        dma((n_kj,)),
        dma((n_kj,)),
        dma((6,)),
        dma((2 * group,)),
        dma((2 * group,)),
        dma((2 * group,)),
        dma((2 * group,)),
        dma((2 * group,)),
        dma((2 * group,)),
    ]
    query_grad, key_grad, value_grad, pair_grad, weights = pl.pallas_call(
        functools.partial(kernel, sizes),
        out_shape=(
            jax.ShapeDtypeStruct((q_half, width), BF16),
            jax.ShapeDtypeStruct((half, width), BF16),
            jax.ShapeDtypeStruct((half, width), BF16),
            jax.ShapeDtypeStruct((count, channels), BF16),
            jax.ShapeDtypeStruct((span, channels), BF16),
        ),
        in_specs=[pl.BlockSpec(memory_space=pl.ANY)] + [vmem] * 10,
        out_specs=(vmem,) * 5,
        scratch_shapes=scratch,
        compiler_params=pltpu.CompilerParams(
            collective_id=0, has_side_effects=True, vmem_limit_bytes=60 * 1024 * 1024
        ),
        name="block_backward",
    )(
        pair_rep,
        query_rows.reshape(rows, width),
        key_rows.reshape(keys, width),
        value_rows.reshape(keys, width),
        output_grad.reshape(rows, width),
        gain_first.reshape(1, channels),
        gate_weight,
        up_weight,
        down_weight,
        gain_second.reshape(1, channels),
        head_weight.T,
    )
    outputs = (query_grad, key_grad, value_grad, pair_grad)
    query_grad, key_grad, value_grad, pair_grad, gate_grad, up_grad, down_grad, head_grad, first_grad, second_grad = pl.pallas_call(
        functools.partial(finish, hidden_count, second_base),
        out_shape=tuple(jax.ShapeDtypeStruct(x.shape, x.dtype) for x in outputs)
        + (
            jax.ShapeDtypeStruct((channels, hidden_count), F32),
            jax.ShapeDtypeStruct((channels, hidden_count), F32),
            jax.ShapeDtypeStruct((hidden_count, channels), F32),
            jax.ShapeDtypeStruct((HEADS, channels), F32),
            jax.ShapeDtypeStruct((1, channels), F32),
            jax.ShapeDtypeStruct((1, channels), F32),
        ),
        in_specs=[vmem] * 5,
        out_specs=(vmem,) * 10,
        name="finish_weights",
    )(weights, *outputs)
    return (
        query_grad[None],
        key_grad[None],
        value_grad[None],
        pair_grad.reshape(1, 1, share, block_count, block_rows, channels),
        gate_grad,
        up_grad,
        down_grad,
        head_grad.T,
        first_grad.reshape(channels),
        second_grad.reshape(channels),
    )


def solution(mesh):
    mesh_shape = (mesh.shape["noise"], mesh.shape["qi"], mesh.shape["kj"])
    return jax.shard_map(
        functools.partial(local, mesh_shape),
        mesh=mesh,
        in_specs=(
            P("qi", None, "kj", None),
            P("noise", "qi", None),
            P("noise", None, "kj", None),
            P("noise", None, "kj", None),
            P("noise", "qi", None),
            P(),
            P(),
            P(),
            P(),
            P(),
            P(),
        ),
        out_specs=(
            P("noise", ("qi", "kj"), None),
            P("noise", ("qi", "kj"), None),
            P("noise", ("qi", "kj"), None),
            P("qi", "noise", None, None, "kj", None),
            P(),
            P(),
            P(),
            P(),
            P(),
            P(),
        ),
        check_vma=False,
    )
```

profile of v0, /device:TPU:0, one launch (start us, length us, event | category | flops | bytes accessed | tf_op | source)
XLA Modules:
  0.0 44.9 jit_solution(15670157805495435231)
XLA Ops:
  0.6 42.1 %block_backward.1 = (bf16[32,768]{1,0:T(8,128)(2,1)}, bf16[32,768]{1,0:T(8,128)(2,1)}, bf16[32,768]{1,0:T(8,128)(2,1)}, bf16[512,128]{1,0:T(8,128)(2,1)}, bf16[1792,128]{1,0:T(8,128)(2,1)}) custom-call(bf16[64,2,32,128]{3,2,1,0:T(8,128)(2,1)} %pair_ref.1, bf16[64,768]{1,0:T(8,128)(2,1)} %bitcast.14, bf16[64,768]{1,0:T(8,128)(2,1)} %bitcast.15, ...), custom_call_target="tpu_custom_call" | custom-call | tf_op jit(solution)/shard_map/block_backward/pallas_call | solution.py:621
  42.8 2.1 %finish_weights.1 = (bf16[32,768]{1,0:T(8,128)(2,1)}, bf16[32,768]{1,0:T(8,128)(2,1)}, bf16[32,768]{1,0:T(8,128)(2,1)}, bf16[512,128]{1,0:T(8,128)(2,1)}, f32[12...) custom-call(bf16[1792,128]{1,0:T(8,128)(2,1)} %get-tuple-element.25., ...), custom_call_target="tpu_custom_call" | custom-call | tf_op jit(solution)/shard_map/finish_weights/pallas_call | solution.py:651
where the time goes:
time: 45.1 us; the launch traced here: 44.9 us
  Pallas kernels  44.2 us (98%)
  between operations  0.65 us (1%)
    pallas_call x1, Pallas kernels, local(): pl.pallas_call(functools.partial(kernel, sizes), out_shape=(jax.ShapeDtyp...  42.1 us
    pallas_call x1, Pallas kernels, local(): pl.pallas_call(functools.partial(finish, hidden_count, second_base), out_...  2.1 us

commit v1 on v0

--- a/solution.py
+++ b/solution.py
@@ -1,4 +1,5 @@
 import functools
+import math
 
 import jax
 import jax.numpy as jnp
@@ -10,6 +11,7 @@
 HEADS = 16
 HEAD_DIM = 48
 ALIGN = 8
+BLOCK = 16
 LANES = 128
 
 epsilon = 1e-05
@@ -36,9 +38,32 @@
     return inverse * (normed_grad - first_mean - normed * second_mean)
 
 
+def place(parts_of, row):
+    wave = 0
+    while row >= parts_of[wave]:
+        row -= parts_of[wave]
+        wave += 1
+    return wave, row
+
+
 def kernel(
     sizes,
-    pair_ref,
+    pair_hbm,
+    q_hbm,
+    k_hbm,
+    v_hbm,
+    g_hbm,
+    gain_first_hbm,
+    gate_hbm,
+    up_hbm,
+    down_hbm,
+    gain_second_hbm,
+    head_hbm,
+    query_out,
+    key_out,
+    value_out,
+    pair_out,
+    tail_out,
     q_ref,
     k_ref,
     v_ref,
@@ -49,11 +74,6 @@
     down_ref,
     gain_second_ref,
     head_ref,
-    query_out,
-    key_out,
-    value_out,
-    pair_out,
-    weight_out,
     cells,
     pre_normed,
     pre_low,
@@ -79,11 +99,9 @@
     query_recv,
     kv_part,
     kv_recv,
-    w_part,
-    w_core,
-    w_sum,
-    w_recv,
-    cell_sem,
+    tail_own,
+    tail_recv,
+    input_sems,
     bias_send_sem,
     bias_recv_sem,
     stat_send_sem,
@@ -99,8 +117,16 @@
     all_recv_sem,
     fwd_send_sem,
     fwd_recv_sem,
+    tail_send_sem,
+    tail_recv_sem,
+    weight_out,
+    w_part,
+    w_core,
+    w_sum,
+    w_recv,
 ):
-    n_noise, n_qi, n_kj, rows, keys, share, blocks = sizes
+    n_noise, n_qi, n_kj, rows, keys, share, parts_of = sizes
+    waves = len(parts_of)
     group = n_noise * n_kj
     cell_count = share * keys
     chunk = min(256, cell_count)
@@ -135,8 +161,26 @@
 
         lax.fori_loop(1, count, step, 0)
 
-    own = pltpu.make_async_copy(pair_ref.at[pl.ds(noise * share, share)], cells, cell_sem)
-    own.start()
+    forward_loads = [
+        pltpu.make_async_copy(src, dst, input_sems.at[i])
+        for i, (src, dst) in enumerate(
+            (
+                (pair_hbm.at[pl.ds(noise * share, share)], cells),
+                (gain_first_hbm, gain_first_ref),
+                (gate_hbm, gate_ref),
+                (up_hbm, up_ref),
+                (down_hbm, down_ref),
+                (gain_second_hbm, gain_second_ref),
+                (head_hbm, head_ref),
+            )
+        )
+    ]
+    attention_loads = [
+        pltpu.make_async_copy(src, dst, input_sems.at[len(forward_loads) + i])
+        for i, (src, dst) in enumerate(((q_hbm, q_ref), (k_hbm, k_ref), (g_hbm, g_ref), (v_hbm, v_ref)))
+    ]
+    for load in forward_loads:
+        load.start()
 
     barrier = pltpu.get_barrier_semaphore()
 
@@ -147,7 +191,10 @@
 
     each(group, greet)
     pl.semaphore_signal(barrier, inc=1, device_id=sibling, device_id_type=MESH)
-    own.wait()
+    for load in attention_loads:
+        load.start()
+    for load in forward_loads:
+        load.wait()
 
     gain_first = gain_first_ref[...]
     gain_second = gain_second_ref[...]
@@ -192,6 +239,8 @@
     def head_of(ref, h):
         return ref[:, h * HEAD_DIM : (h + 1) * HEAD_DIM]
 
+    for load in attention_loads:
+        load.wait()
     for h in range(HEADS):
         score[h] = dot(head_of(q_ref, h), head_of(k_ref, h), 1, 1) * scale
         attend_grad[h] = dot(head_of(g_ref, h), head_of(v_ref, h), 1, 1)
@@ -202,7 +251,9 @@
 
     hidden_t[...] = hidden[...].T
     pre_low_t[...] = pre_low[...].T
-    w_part[...] = jnp.zeros(w_part.shape, BF16)
+    for wave, part in enumerate(parts_of):
+        if part < math.prod(w_part[wave].shape[:3]):
+            w_part[wave][...] = jnp.zeros(w_part[wave].shape, BF16)
     each(n_noise, bias_wait)
 
     for h in range(HEADS):
@@ -305,15 +356,15 @@
         head_part += dot(grad_low, post_low[at], 1, 0)
     hidden_count = gate_ref.shape[1]
     tiles = hidden_count // channels
-    split = 3 * tiles // 2
-    span = [group * part for part in blocks]
-    base = [0, n_qi * span[0]]
-    half_base = [0, span[0]]
-    block_base = [0, blocks[0]]
 
     def put(t, value):
-        first = t * channels if t < split else base[1] + (t - split) * channels
-        w_part[first : first + channels] = value.astype(BF16)
+        wave, first = place(parts_of, t * channels)
+        block = w_part[wave].shape[2]
+        count = channels // block
+        owner = first // block
+        w_part[wave][owner // group, owner % group : owner % group + count] = value.astype(BF16).reshape(
+            count, block, channels
+        )
 
     starts = range(0, cell_count, chunk)
     second_part = jnp.zeros((1, channels), F32)
@@ -339,22 +390,13 @@
         put(t, down_part[at])
         put(tiles + t, gate_part[:, at])
 
-    def half_rows(wave, core):
-        return pl.ds(pl.multiple_of(base[wave] + core * span[wave], ALIGN), span[wave])
-
-    def sum_rows(wave):
-        return pl.ds(half_base[wave], span[wave])
-
     def core_copy(wave):
         return remote(
-            w_part.at[half_rows(wave, 1 - qi)],
-            w_core.at[sum_rows(wave)],
-            pair_sems.at[2 + 2 * wave],
-            pair_sems.at[3 + 2 * wave],
-            sibling,
-        )
-
-    core_copy(0).start()
+            w_part[wave].at[1 - qi], w_core[wave], pair_sems.at[2 + 2 * wave], pair_sems.at[3 + 2 * wave], sibling
+        )
+
+    if waves > 1:
+        core_copy(0).start()
 
     first_part = jnp.zeros((1, channels), F32)
     up_part = jnp.zeros((channels, hidden_count), F32)
@@ -366,60 +408,52 @@
         post_normed[at] = pre_scaled
     for t in range(tiles):
         put(2 * tiles + t, up_part[:, t * channels : (t + 1) * channels])
-    tail = base[1] + (3 * tiles - split) * channels
-    w_part[tail : tail + HEADS] = head_part.astype(BF16)
-    w_part[tail + HEADS : tail + 2 * HEADS] = jnp.concatenate(
-        (
-            jnp.broadcast_to(first_part, (HEADS // 2, channels)),
-            jnp.broadcast_to(second_part, (HEADS // 2, channels)),
-        ),
-        0,
-    ).astype(BF16)
-    core_copy(1).start()
-
-    def own_rows(wave, index):
-        return pl.ds(pl.multiple_of(half_base[wave] + index * blocks[wave], ALIGN), blocks[wave])
+    core_copy(waves - 1).start()
+
+    tail_own[0, 0:HEADS] = head_part
+    tail_own[0, HEADS : HEADS + 1] = first_part
+    tail_own[0, HEADS + 1 : HEADS + 2] = second_part
+    tail_own[0, HEADS + 2 :] = jnp.zeros((ALIGN - 2, channels), F32)
+    tail_steps = tail_own.shape[0] - 1
+
+    def tail_copy(step):
+        peer = sibling if step == 0 else of_group(lax.bitwise_xor(me, 1 << (step - 1)))
+        return remote(
+            tail_own.at[step], tail_recv.at[step], tail_send_sem.at[step], tail_recv_sem.at[step], peer
+        )
+
+    def tail_next(step):
+        tail_copy(step).wait_recv()
+        tail_own[step + 1] = tail_own[step] + tail_recv[step]
+        if step + 1 < tail_steps:
+            tail_copy(step + 1).start()
+
+    tail_copy(0).start()
 
     def w_copy(wave, slot, peer):
         return remote(
-            w_sum.at[own_rows(wave, peer)],
-            w_recv.at[slot, pl.ds(block_base[wave], blocks[wave])],
+            w_sum[wave].at[peer],
+            w_recv[wave].at[slot],
             w_send_sem.at[wave * group + peer],
             w_recv_sem.at[wave * group + slot],
             of_group(peer),
         )
 
-    def out_rows(wave, core, index):
-        return pl.ds(
-            pl.multiple_of(base[wave] + core * span[wave] + index * blocks[wave], ALIGN), blocks[wave]
-        )
-
     def all_copy(wave, slot, peer):
-        at = out_rows(wave, qi, slot)
+        at = weight_out[wave].at[qi, slot]
         return remote(
-            weight_out.at[at],
-            weight_out.at[at],
-            all_send_sem.at[wave * group + peer],
-            all_recv_sem.at[wave * group + slot],
-            of_group(peer),
-        )
-
-    def fwd_copy(wave, core, slot):
-        at = out_rows(wave, core, slot)
-        return remote(
-            weight_out.at[at],
-            weight_out.at[at],
-            fwd_send_sem.at[wave * group + slot],
-            fwd_recv_sem.at[wave * group + slot],
-            sibling,
-        )
-
-    for wave in range(2):
+            at, at, all_send_sem.at[wave * group + peer], all_recv_sem.at[wave * group + slot], of_group(peer)
+        )
+
+    def fwd_copy(wave, core):
+        at = weight_out[wave].at[core]
+        return remote(at, at, fwd_send_sem.at[wave], fwd_recv_sem.at[wave], sibling)
+
+    for wave in range(waves):
         core_copy(wave).wait_recv()
-        w_sum[sum_rows(wave)] = (
-            w_part[half_rows(wave, qi)].astype(F32) + w_core[sum_rows(wave)].astype(F32)
-        ).astype(BF16)
+        w_sum[wave][...] = (w_part[wave][qi].astype(F32) + w_core[wave][...].astype(F32)).astype(BF16)
         each(group, lambda i: w_copy(wave, me, lax.rem(me + i, group)).start())
+    tail_next(0)
 
     for start in starts:
         at = slice(start, start + chunk)
@@ -439,35 +473,36 @@
     key_out[...] = kv_total[:, :width].astype(BF16)
     value_out[...] = kv_total[:, width:].astype(BF16)
 
-    for wave in range(2):
+    for wave in range(waves):
 
         def w_add(i, total):
             peer = lax.rem(me + group - i, group)
             w_copy(wave, peer, peer).wait_recv()
-            return total + w_recv[peer, pl.ds(block_base[wave], blocks[wave])].astype(F32)
-
-        total = lax.fori_loop(1, group, w_add, w_sum[own_rows(wave, me)].astype(F32))
-        weight_out[out_rows(wave, qi, me)] = (total * (1.0 / (rows * n_qi))).astype(BF16)
+            return total + w_recv[wave][peer].astype(F32)
+
+        total = lax.fori_loop(1, group, w_add, w_sum[wave][me].astype(F32))
+        weight_out[wave][qi, me] = (total * (1.0 / (rows * n_qi))).astype(BF16)
         each(group, lambda i: all_copy(wave, me, lax.rem(me + i, group)).start())
-        fwd_copy(wave, qi, me).start()
-
-    for wave in range(2):
-
-        def forward(i):
+        if 1 + wave < tail_steps:
+            tail_next(1 + wave)
+
+    for wave in range(waves):
+
+        def all_wait(i):
             peer = lax.rem(me + group - i, group)
             all_copy(wave, peer, peer).wait_recv()
-            fwd_copy(wave, qi, peer).start()
-
-        each(group, forward)
-
-    for wave in range(2):
-
-        def fwd_wait(i, carry):
-            fwd_copy(wave, 1 - qi, i).wait_recv()
-            fwd_copy(wave, qi, i).wait_send()
-            return carry
-
-        lax.fori_loop(0, group, fwd_wait, 0)
+
+        each(group, all_wait)
+        fwd_copy(wave, qi).start()
+        if 1 + waves + wave < tail_steps:
+            tail_next(1 + waves + wave)
+    for step in range(1 + 2 * waves, tail_steps):
+        tail_next(step)
+    tail_out[...] = tail_own[tail_steps] * (1.0 / (rows * n_qi))
+
+    for wave in range(waves):
+        fwd_copy(wave, 1 - qi).wait_recv()
+        fwd_copy(wave, qi).wait_send()
 
         def drain(i):
             peer = lax.rem(me + i, group)
@@ -476,6 +511,8 @@
 
         each(group, drain)
         core_copy(wave).wait_send()
+    for step in range(tail_steps):
+        tail_copy(step).wait_send()
 
     def drain_noise(i):
         peer = lax.rem(noise + i, n_noise)
@@ -495,8 +532,9 @@
 
 def finish(
     hidden_count,
-    second_base,
-    weight_ref,
+    parts_of,
+    group,
+    tail_ref,
     query_ref,
     key_ref,
     value_ref,
@@ -511,29 +549,52 @@
     head_out,
     first_out,
     second_out,
+    gate_wide,
+    up_wide,
+    down_wide,
+    first_wide,
+    second_wide,
+    sems,
+    weight_ref,
 ):
-    query_out[...] = query_ref[...]
-    key_out[...] = key_ref[...]
-    value_out[...] = value_ref[...]
-    pair_out[...] = pair_ref[...]
-    channels = weight_ref.shape[1]
+    copies = []
+
+    def store(src, dst):
+        copy = pltpu.make_async_copy(src, dst, sems.at[len(copies)])
+        copy.start()
+        copies.append(copy)
+
+    store(pair_ref, pair_out)
+    store(query_ref, query_out)
+    store(key_ref, key_out)
+    store(value_ref, value_out)
+    channels = tail_ref.shape[1]
     tiles = hidden_count // channels
-    split = 3 * tiles // 2
 
     def tile(t):
-        first = t * channels if t < split else second_base + (t - split) * channels
-        return weight_ref[first : first + channels].astype(F32)
+        wave, first = place(parts_of, t * channels)
+        block = weight_ref[wave].shape[2]
+        count = channels // block
+        owner = first // block
+        value = weight_ref[wave][owner // group, owner % group : owner % group + count]
+        return value.astype(F32).reshape(channels, channels)
 
     for t in range(tiles):
-        at = slice(t * channels, (t + 1) * channels)
-        down_out[at] = tile(t)
-        gate_out[:, at] = tile(tiles + t)
-        up_out[:, at] = tile(2 * tiles + t)
-    tail = second_base + (3 * tiles - split) * channels
-    head_out[...] = weight_ref[tail : tail + HEADS].astype(F32)
-    small = weight_ref[tail + HEADS : tail + 2 * HEADS].astype(F32)
-    first_out[...] = small[0:1]
-    second_out[...] = small[HEADS // 2 : HEADS // 2 + 1]
+        down_wide[t * channels : (t + 1) * channels] = tile(t)
+    store(down_wide, down_out)
+    for t in range(tiles):
+        gate_wide[:, t * channels : (t + 1) * channels] = tile(tiles + t)
+    store(gate_wide, gate_out)
+    for t in range(tiles):
+        up_wide[:, t * channels : (t + 1) * channels] = tile(2 * tiles + t)
+    store(up_wide, up_out)
+    store(tail_ref.at[pl.ds(0, HEADS)], head_out)
+    first_wide[...] = tail_ref[HEADS : HEADS + 1]
+    second_wide[...] = tail_ref[HEADS + 1 : HEADS + 2]
+    store(first_wide, first_out)
+    store(second_wide, second_out)
+    for copy in copies:
+        copy.wait()
 
 
 def local(
@@ -558,20 +619,34 @@
     count = share * keys
     group = n_noise * n_kj
     hidden_count = gate_weight.shape[1]
-    split = 3 * (hidden_count // channels) // 2 * channels
-    wave_rows = (split, 3 * hidden_count - split + 2 * HEADS)
-    blocks = tuple(-(-part // (n_qi * group * ALIGN)) * ALIGN for part in wave_rows)
-    block = sum(blocks)
-    second_base = n_qi * group * blocks[0]
+    devices = n_qi * group
+    if hidden_count % (BLOCK * devices) == 0:
+        parts_of = (2 * hidden_count, hidden_count)
+    else:
+        parts_of = (3 * hidden_count,)
+    waves = tuple(
+        (n_qi, group, -(-part // (BLOCK * devices)) * BLOCK, channels) for part in parts_of
+    )
+    tail_shape = (HEADS + ALIGN, channels)
+    tail_steps = 1 + (group - 1).bit_length()
     half = keys // n_qi
     q_half = rows // n_kj
-    sizes = (n_noise, n_qi, n_kj, rows, keys, share, blocks)
+    sizes = (n_noise, n_qi, n_kj, rows, keys, share, parts_of)
     pack = max(1, LANES // keys)
     vmem = pl.BlockSpec(memory_space=pltpu.VMEM)
     dma = pltpu.SemaphoreType.DMA
-    span = n_qi * group * block
 
     scratch = [
+        pltpu.VMEM((rows, width), BF16),
+        pltpu.VMEM((keys, width), BF16),
+        pltpu.VMEM((keys, width), BF16),
+        pltpu.VMEM((rows, width), BF16),
+        pltpu.VMEM((1, channels), F32),
+        pltpu.VMEM((channels, hidden_count), BF16),
+        pltpu.VMEM((channels, hidden_count), BF16),
+        pltpu.VMEM((hidden_count, channels), BF16),
+        pltpu.VMEM((1, channels), F32),
+        pltpu.VMEM((HEADS, channels), BF16),
         pltpu.VMEM((share, block_count, block_rows, channels), BF16),
         pltpu.VMEM((count, channels), F32),
         pltpu.VMEM((count, channels), BF16),
@@ -597,11 +672,9 @@
         pltpu.VMEM((n_kj, q_half, width), BF16),
         pltpu.VMEM((n_qi, half, 2 * width), BF16),
         pltpu.VMEM((half, 2 * width), BF16),
-        pltpu.VMEM((span, channels), BF16),
-        pltpu.VMEM((group * block, channels), BF16),
-        pltpu.VMEM((group * block, channels), BF16),
-        pltpu.VMEM((group, block, channels), BF16),
-        dma(()),
+        pltpu.VMEM((1 + tail_steps, *tail_shape), F32),
+        pltpu.VMEM((tail_steps, *tail_shape), F32),
+        dma((11,)),
         dma((n_noise,)),
         dma((n_noise,)),
         dma((n_kj,)),
@@ -611,45 +684,74 @@
         dma((n_kj,)),
         dma((n_kj,)),
         dma((6,)),
-        dma((2 * group,)),
-        dma((2 * group,)),
-        dma((2 * group,)),
-        dma((2 * group,)),
-        dma((2 * group,)),
-        dma((2 * group,)),
+        dma((len(waves) * group,)),
+        dma((len(waves) * group,)),
+        dma((len(waves) * group,)),
+        dma((len(waves) * group,)),
+        dma((len(waves),)),
+        dma((len(waves),)),
+        dma((tail_steps,)),
+        dma((tail_steps,)),
     ]
-    query_grad, key_grad, value_grad, pair_grad, weights = pl.pallas_call(
-        functools.partial(kernel, sizes),
+    wave_scratch = [
+        [pltpu.VMEM(wave[skip:], BF16) for wave in waves] for skip in (0, 1, 1, 1)
+    ]
+    scratch += sum(wave_scratch, [])
+
+    def run(*refs):
+        count = len(waves)
+        outs = refs[16 : 16 + count]
+        rest = refs[16 + count :]
+        groups = [rest[len(rest) - (4 - i) * count : len(rest) - (3 - i) * count] for i in range(4)]
+        kernel(sizes, *refs[:16], *rest[: len(rest) - 4 * count], outs, *groups)
+
+    held = sum(
+        math.prod(x.shape) * jnp.dtype(x.dtype).itemsize for x in scratch if x.memory_space == pltpu.VMEM
+    )
+    hbm = pl.BlockSpec(memory_space=pltpu.HBM)
+    query_grad, key_grad, value_grad, pair_grad, tail, *weights = pl.pallas_call(
+        run,
         out_shape=(
             jax.ShapeDtypeStruct((q_half, width), BF16),
             jax.ShapeDtypeStruct((half, width), BF16),
             jax.ShapeDtypeStruct((half, width), BF16),
             jax.ShapeDtypeStruct((count, channels), BF16),
-            jax.ShapeDtypeStruct((span, channels), BF16),
+            jax.ShapeDtypeStruct(tail_shape, F32),
+            *(jax.ShapeDtypeStruct(wave, BF16) for wave in waves),
         ),
-        in_specs=[pl.BlockSpec(memory_space=pl.ANY)] + [vmem] * 10,
-        out_specs=(vmem,) * 5,
+        in_specs=[hbm] * 11,
+        out_specs=(vmem,) * (5 + len(waves)),
         scratch_shapes=scratch,
         compiler_params=pltpu.CompilerParams(
-            collective_id=0, has_side_effects=True, vmem_limit_bytes=60 * 1024 * 1024
+            collective_id=0, has_side_effects=True, vmem_limit_bytes=held + held // 8 + 4 * 1024 * 1024
         ),
         name="block_backward",
     )(
-        pair_rep,
-        query_rows.reshape(rows, width),
-        key_rows.reshape(keys, width),
-        value_rows.reshape(keys, width),
-        output_grad.reshape(rows, width),
-        gain_first.reshape(1, channels),
-        gate_weight,
-        up_weight,
-        down_weight,
-        gain_second.reshape(1, channels),
-        head_weight.T,
+        *(
+            pltpu.with_memory_space_constraint(x, pltpu.HBM)
+            for x in (
+                pair_rep,
+                query_rows.reshape(rows, width),
+                key_rows.reshape(keys, width),
+                value_rows.reshape(keys, width),
+                output_grad.reshape(rows, width),
+                gain_first.reshape(1, channels),
+                gate_weight,
+                up_weight,
+                down_weight,
+                gain_second.reshape(1, channels),
+                head_weight.T,
+            )
+        )
     )
     outputs = (query_grad, key_grad, value_grad, pair_grad)
+
+    def finish_all(*refs):
+        count = len(waves)
+        finish(hidden_count, parts_of, group, *refs[:5], *refs[5 + count :], refs[5 : 5 + count])
+
     query_grad, key_grad, value_grad, pair_grad, gate_grad, up_grad, down_grad, head_grad, first_grad, second_grad = pl.pallas_call(
-        functools.partial(finish, hidden_count, second_base),
+        finish_all,
         out_shape=tuple(jax.ShapeDtypeStruct(x.shape, x.dtype) for x in outputs)
         + (
             jax.ShapeDtypeStruct((channels, hidden_count), F32),
@@ -659,10 +761,19 @@
             jax.ShapeDtypeStruct((1, channels), F32),
             jax.ShapeDtypeStruct((1, channels), F32),
         ),
-        in_specs=[vmem] * 5,
-        out_specs=(vmem,) * 10,
+        in_specs=[vmem] * (5 + len(waves)),
+        out_specs=(hbm,) * 10,
+        scratch_shapes=[
+            pltpu.VMEM((channels, hidden_count), F32),
+            pltpu.VMEM((channels, hidden_count), F32),
+            pltpu.VMEM((hidden_count, channels), F32),
+            pltpu.VMEM((1, channels), F32),
+            pltpu.VMEM((1, channels), F32),
+            dma((10,)),
+        ],
+        compiler_params=pltpu.CompilerParams(vmem_limit_bytes=8 * 1024 * 1024),
         name="finish_weights",
-    )(weights, *outputs)
+    )(tail, *outputs, *weights)
     return (
         query_grad[None],
         key_grad[None],

time: 45.1 us -> 42.9 us (0.951)
  Pallas kernels: 44.2 us -> 42.1 us
    pallas_call x2, Pallas kernels: 44.2 us -> 42.1 us  [the longest x1 41 us: local(): pl.pallas_call(run, out_shape=(jax.ShapeDtypeStruct((q_half, width), BF16...]
where the time goes in v1:
time: 42.9 us; the launch traced here: 42.8 us
  Pallas kernels  42.1 us (98%)
  between operations  0.65 us (2%)
    pallas_call x1, Pallas kernels, local(): pl.pallas_call(run, out_shape=(jax.ShapeDtypeStruct((q_half, width), BF16...  41 us
    pallas_call x1, Pallas kernels, local(): pl.pallas_call(finish_all, out_shape=tuple((jax.ShapeDtypeStruct(x.shape,...  1.07 us

profile of v1, /device:TPU:0, one launch (start us, length us, event | category | flops | bytes accessed | tf_op | source)
XLA Modules:
  0.0 42.8 jit_solution(11304107917250424749)
XLA Ops:
  0.6 41.0 %block_backward.1 = (bf16[32,768]{1,0:T(8,128)(2,1)S(1)}, bf16[32,768]{1,0:T(8,128)(2,1)S(1)}, bf16[32,768]{1,0:T(8,128)(2,1)S(1)}, bf16[512,128]{1,0:T(8,128)(2...) custom-call(bf16[64,2,32,128]{3,2,1,0:T(8,128)(2,1)} %refs_0_.1, ...), custom_call_target="tpu_custom_call" | custom-call | tf_op jit(solution)/shard_map/block_backward/pallas_call | solution.py:712
  41.7 1.1 %finish_weights.1 = (bf16[32,768]{1,0:T(8,128)(2,1)}, bf16[32,768]{1,0:T(8,128)(2,1)}, bf16[32,768]{1,0:T(8,128)(2,1)}, bf16[512,128]{1,0:T(8,128)(2,1)}, f32[12...) custom-call(f32[24,128]{1,0:T(8,128)S(1)} %get-tuple-element.27.refs, ...), custom_call_target="tpu_custom_call" | custom-call | tf_op jit(solution)/shard_map/finish_weights/pallas_call | solution.py:753

commit v2 on v1

--- a/solution.py
+++ b/solution.py
@@ -87,10 +87,20 @@
     post_low,
     inverses,
     bias_rows,
+    bias_send,
     bias_all,
+    q_cols,
+    g_cols,
+    kv_send,
+    kv_all,
+    q_heads,
+    g_heads,
+    k_heads,
     score,
     attend_grad,
-    stats,
+    score_low,
+    attend_low,
+    score_cat,
     grad_send,
     grad_recv,
     grad_sum,
@@ -99,17 +109,21 @@
     query_recv,
     kv_part,
     kv_recv,
-    tail_own,
+    tail_part,
+    tail_core,
+    tail_sum,
     tail_recv,
     input_sems,
     bias_send_sem,
     bias_recv_sem,
-    stat_send_sem,
-    stat_recv_sem,
+    tile_send_sem,
+    tile_recv_sem,
     grad_send_sem,
     grad_recv_sem,
     query_send_sem,
     query_recv_sem,
+    kv_send_sem,
+    kv_recv_sem,
     pair_sems,
     w_send_sem,
     w_recv_sem,
@@ -117,6 +131,7 @@
     all_recv_sem,
     fwd_send_sem,
     fwd_recv_sem,
+    tail_sems,
     tail_send_sem,
     tail_recv_sem,
     weight_out,
@@ -140,8 +155,10 @@
     width = q_ref.shape[-1]
     half = keys // n_qi
     q_half = rows // n_kj
-    pack = max(1, LANES // keys)
-    packed = HEADS // pack
+    own = HEADS // n_kj
+    part = own * HEAD_DIM
+    pack = min(own, max(1, LANES // keys))
+    packed = own // pack
 
     def members(p):
         return [p + j * packed for j in range(pack)]
@@ -224,134 +241,149 @@
         inverses[at, 1:2] = after_inverse
     for i in range(share):
         bias_rows[i] = dot(head_t, post_low[i * keys : (i + 1) * keys], 1, 1)
-    for p in range(packed):
-        bias_all[noise, p] = jnp.concatenate([bias_rows[:, h, :] for h in members(p)], 1).astype(BF16)
+    for j in range(n_kj):
+        for p in range(packed):
+            bias_send[j, p] = jnp.concatenate([bias_rows[:, j * own + h, :] for h in members(p)], 1).astype(BF16)
+
+    for load in attention_loads:
+        load.wait()
+    for j in range(n_kj):
+        at = slice(j * part, (j + 1) * part)
+        q_cols[j] = q_ref[:, at]
+        g_cols[j] = g_ref[:, at]
+        kv_send[j, 0] = k_ref[:, at]
+        kv_send[j, 1] = v_ref[:, at]
 
     pl.semaphore_wait(barrier, group)
+
+    def tile_copy(slot, peer):
+        return remote(
+            kv_send.at[peer], kv_all.at[slot], tile_send_sem.at[peer], tile_recv_sem.at[slot], {"kj": peer}
+        )
 
     def bias_copy(slot, peer):
         return remote(
-            bias_all.at[slot], bias_all.at[slot], bias_send_sem.at[peer], bias_recv_sem.at[slot], {"noise": peer}
-        )
-
-    each(n_noise, lambda i: bias_copy(noise, lax.rem(noise + i, n_noise)).start())
-
-    def head_of(ref, h):
-        return ref[:, h * HEAD_DIM : (h + 1) * HEAD_DIM]
-
-    for load in attention_loads:
-        load.wait()
-    for h in range(HEADS):
-        score[h] = dot(head_of(q_ref, h), head_of(k_ref, h), 1, 1) * scale
-        attend_grad[h] = dot(head_of(g_ref, h), head_of(v_ref, h), 1, 1)
-
-    def bias_wait(i):
-        peer = lax.rem(noise + n_noise - i, n_noise)
-        bias_copy(peer, peer).wait_recv()
-
+            bias_send.at[lax.rem(peer, n_kj)],
+            bias_all.at[slot],
+            bias_send_sem.at[peer],
+            bias_recv_sem.at[slot],
+            of_group(peer),
+        )
+
+    each(n_kj, lambda i: tile_copy(kj, lax.rem(kj + i, n_kj)).start())
+    each(group, lambda i: bias_copy(me, lax.rem(me + i, group)).start())
+
+    kv_all[kj] = kv_send[kj]
+    bias_all[me] = bias_send[kj]
+    lane = lax.broadcasted_iota(jnp.int32, (1, part), 1)
+
+    def mask(h):
+        inside = jnp.logical_and(lane >= h * HEAD_DIM, lane < (h + 1) * HEAD_DIM)
+        return jnp.where(inside, 1.0, 0.0).astype(BF16)
+
+    q_own = q_cols[kj]
+    g_own = g_cols[kj]
+    for h in range(own):
+        at = slice(h * rows, (h + 1) * rows)
+        q_heads[at] = q_own * mask(h)
+        g_heads[at] = g_own * mask(h)
     hidden_t[...] = hidden[...].T
     pre_low_t[...] = pre_low[...].T
-    for wave, part in enumerate(parts_of):
-        if part < math.prod(w_part[wave].shape[:3]):
+    for wave, count in enumerate(parts_of):
+        if count < math.prod(w_part[wave].shape[:3]):
             w_part[wave][...] = jnp.zeros(w_part[wave].shape, BF16)
-    each(n_noise, bias_wait)
-
-    for h in range(HEADS):
-        bias_at = slice(h // packed * keys, (h // packed + 1) * keys)
-        full = score[h] + bias_all[:, h % packed].astype(F32).reshape(rows, pack * keys)[:, bias_at]
-        largest = jnp.max(full, axis=1, keepdims=True)
-        expo = jnp.exp(full - largest)
-        score[h] = expo
-        stats[kj, :, h : h + 1] = largest
-        stats[kj, :, HEADS + h : HEADS + h + 1] = jnp.sum(expo, axis=1, keepdims=True)
-        stats[kj, :, 2 * HEADS + h : 2 * HEADS + h + 1] = jnp.sum(
-            expo * attend_grad[h], axis=1, keepdims=True
-        )
-
-    def stat_copy(slot, peer):
-        return remote(
-            stats.at[slot], stats.at[slot], stat_send_sem.at[peer], stat_recv_sem.at[slot], {"kj": peer}
-        )
-
-    each(n_kj, lambda i: stat_copy(kj, lax.rem(kj + i, n_kj)).start())
-
-    def stat_wait(i):
+
+    def tile_wait(i):
         peer = lax.rem(kj + n_kj - i, n_kj)
-        stat_copy(peer, peer).wait_recv()
-
-    each(n_kj, stat_wait)
-
-    parts = [stats[j] for j in range(n_kj)]
-    row_max = parts[0][:, 0:HEADS]
-    for part in parts[1:]:
-        row_max = jnp.maximum(row_max, part[:, 0:HEADS])
-    row_sum = jnp.zeros_like(row_max)
-    row_dot = jnp.zeros_like(row_max)
-    for part in parts:
-        weight = jnp.exp(part[:, 0:HEADS] - row_max)
-        row_sum += weight * part[:, HEADS : 2 * HEADS]
-        row_dot += weight * part[:, 2 * HEADS : 3 * HEADS]
-    factor = jnp.exp(stats[kj, :, 0:HEADS] - row_max) / row_sum
-    delta = row_dot / row_sum
+        tile_copy(peer, peer).wait_recv()
+
+    each(n_kj, tile_wait)
+    k_own = kv_all[:, 0].reshape(n_kj * keys, part)
+    v_own = kv_all[:, 1].reshape(n_kj * keys, part)
+    score[...] = dot(q_heads[...], k_own, 1, 1) * scale
+    attend_grad[...] = dot(g_heads[...], v_own, 1, 1)
+    for h in range(own):
+        k_heads[h * n_kj * keys : (h + 1) * n_kj * keys] = k_own * mask(h)
+
+    def bias_wait(i):
+        peer = lax.rem(me + group - i, group)
+        bias_copy(peer, peer).wait_recv()
+
+    each(group, bias_wait)
+
     for p in range(packed):
-        pieces = []
-        for h in members(p):
-            attend = score[h] * factor[:, h : h + 1]
-            score_grad = attend * (attend_grad[h] - delta[:, h : h + 1])
-            score[h] = attend
-            attend_grad[h] = score_grad
-            pieces.append(score_grad)
-        grad_send[:, p] = jnp.concatenate(pieces, 1).reshape(n_noise, share, pack * keys).astype(BF16)
+        blocks = [
+            jnp.concatenate([bias_all[n * n_kj + j, p] for n in range(n_noise)], 0).astype(F32) for j in range(n_kj)
+        ]
+        grads = []
+        for i, h in enumerate(members(p)):
+            at = slice(h * rows, (h + 1) * rows)
+            full = score[at] + jnp.concatenate([block[:, i * keys : (i + 1) * keys] for block in blocks], 1)
+            expo = jnp.exp(full - jnp.max(full, axis=1, keepdims=True))
+            attend = expo * (1.0 / jnp.sum(expo, axis=1, keepdims=True))
+            weighed = attend_grad[at]
+            score_grad = attend * (weighed - jnp.sum(attend * weighed, axis=1, keepdims=True))
+            grads.append(score_grad)
+            attend_low[at] = attend.astype(BF16)
+            score_low[at] = score_grad.astype(BF16)
+            score_cat[:, h * n_kj * keys : (h + 1) * n_kj * keys] = score_grad.astype(BF16)
+        for j in range(n_kj):
+            piece = jnp.concatenate([grad[:, j * keys : (j + 1) * keys] for grad in grads], 1).astype(BF16)
+            for n in range(n_noise):
+                grad_send[n * n_kj + j, p] = piece[n * share : (n + 1) * share]
 
     def grad_copy(slot, peer):
         return remote(
-            grad_send.at[peer], grad_recv.at[slot], grad_send_sem.at[peer], grad_recv_sem.at[slot], {"noise": peer}
-        )
-
-    each(n_noise, lambda i: grad_copy(noise, lax.rem(noise + i, n_noise)).start())
-
-    for h in range(HEADS):
-        at = slice(h * HEAD_DIM, (h + 1) * HEAD_DIM)
-        value_at = slice(width + h * HEAD_DIM, width + (h + 1) * HEAD_DIM)
-        score_low = attend_grad[h].astype(BF16)
-        attend_low = score[h].astype(BF16)
-        query_part[:, :, at] = (
-            (dot(score_low, head_of(k_ref, h), 1, 0) * scale).astype(BF16).reshape(n_kj, q_half, HEAD_DIM)
-        )
-        kv_part[:, :, at] = (
-            (dot(score_low, head_of(q_ref, h), 0, 0) * scale).astype(BF16).reshape(n_qi, half, HEAD_DIM)
-        )
-        kv_part[:, :, value_at] = (
-            dot(attend_low, head_of(g_ref, h), 0, 0).astype(BF16).reshape(n_qi, half, HEAD_DIM)
-        )
+            grad_send.at[peer], grad_recv.at[slot], grad_send_sem.at[peer], grad_recv_sem.at[slot], of_group(peer)
+        )
+
+    each(group, lambda i: grad_copy(me, lax.rem(me + i, group)).start())
+
+    query_all = (dot(score_cat[...], k_heads[...], 1, 0) * scale).astype(BF16)
+    for j in range(n_kj):
+        query_part[j] = query_all[j * q_half : (j + 1) * q_half]
+    key_all = (dot(score_low[...], q_heads[...], 0, 0) * scale).astype(BF16)
+    value_all = dot(attend_low[...], g_heads[...], 0, 0).astype(BF16)
+    for j in range(n_kj):
+        for i in range(n_qi):
+            at = slice(j * keys + i * half, j * keys + (i + 1) * half)
+            kv_part[i * n_kj + j, 0] = key_all[at]
+            kv_part[i * n_kj + j, 1] = value_all[at]
 
     def query_copy(slot, peer):
         return remote(
             query_part.at[peer], query_recv.at[slot], query_send_sem.at[peer], query_recv_sem.at[slot], {"kj": peer}
         )
 
+    def kv_copy(slot, peer):
+        device = {"qi": peer // n_kj, "kj": lax.rem(peer, n_kj)}
+        return remote(kv_part.at[peer], kv_recv.at[slot], kv_send_sem.at[peer], kv_recv_sem.at[slot], device)
+
+    cell = qi * n_kj + kj
     each(n_kj, lambda i: query_copy(kj, lax.rem(kj + i, n_kj)).start())
-    kv_copy = remote(kv_part.at[1 - qi], kv_recv, pair_sems.at[0], pair_sems.at[1], sibling)
-    kv_copy.start()
+    each(n_qi * n_kj, lambda i: kv_copy(cell, lax.rem(cell + i, n_qi * n_kj)).start())
+    query_recv[kj] = query_part[kj]
+    kv_recv[cell] = kv_part[cell]
+
+    grad_recv[me] = grad_send[me]
 
     def grad_wait(i):
-        peer = lax.rem(noise + n_noise - i, n_noise)
+        peer = lax.rem(me + group - i, group)
         grad_copy(peer, peer).wait_recv()
 
-    grad_sum[...] = grad_send[noise].astype(F32)
-
-    def grad_add(i):
-        grad_wait(i)
-        peer = lax.rem(noise + n_noise - i, n_noise)
-        grad_sum[...] += grad_recv[peer].astype(F32)
-
-    each(n_noise, grad_add)
+    each(group, grad_wait)
+    for j in range(n_kj):
+        total = grad_recv[j].astype(F32)
+        for n in range(1, n_noise):
+            total += grad_recv[n * n_kj + j].astype(F32)
+        grad_sum[j] = total
 
     head_part = jnp.zeros((HEADS, channels), F32)
     for i in range(share):
         at = slice(i * keys, (i + 1) * keys)
-        grad_row = grad_sum[:, i, :]
-        grad_low = jnp.concatenate([grad_row[:, j * keys : (j + 1) * keys] for j in range(pack)], 0).astype(BF16)
+        grad_low = jnp.concatenate(
+            [grad_sum[j, :, i, m * keys : (m + 1) * keys] for j in range(n_kj) for m in range(pack)], 0
+        ).astype(BF16)
         post_scaled[at] = dot(grad_low, head_t, 0, 0)
         head_part += dot(grad_low, post_low[at], 1, 0)
     hidden_count = gate_ref.shape[1]
@@ -392,7 +424,7 @@
 
     def core_copy(wave):
         return remote(
-            w_part[wave].at[1 - qi], w_core[wave], pair_sems.at[2 + 2 * wave], pair_sems.at[3 + 2 * wave], sibling
+            w_part[wave].at[1 - qi], w_core[wave], pair_sems.at[2 * wave], pair_sems.at[2 * wave + 1], sibling
         )
 
     if waves > 1:
@@ -410,25 +442,24 @@
         put(2 * tiles + t, up_part[:, t * channels : (t + 1) * channels])
     core_copy(waves - 1).start()
 
-    tail_own[0, 0:HEADS] = head_part
-    tail_own[0, HEADS : HEADS + 1] = first_part
-    tail_own[0, HEADS + 1 : HEADS + 2] = second_part
-    tail_own[0, HEADS + 2 :] = jnp.zeros((ALIGN - 2, channels), F32)
-    tail_steps = tail_own.shape[0] - 1
-
-    def tail_copy(step):
-        peer = sibling if step == 0 else of_group(lax.bitwise_xor(me, 1 << (step - 1)))
-        return remote(
-            tail_own.at[step], tail_recv.at[step], tail_send_sem.at[step], tail_recv_sem.at[step], peer
-        )
-
-    def tail_next(step):
-        tail_copy(step).wait_recv()
-        tail_own[step + 1] = tail_own[step] + tail_recv[step]
-        if step + 1 < tail_steps:
-            tail_copy(step + 1).start()
-
-    tail_copy(0).start()
+    tail_part[0:HEADS] = head_part.astype(BF16)
+    tail_part[HEADS:] = jnp.concatenate(
+        (
+            jnp.broadcast_to(first_part, (ALIGN // 2, channels)),
+            jnp.broadcast_to(second_part, (ALIGN // 2, channels)),
+        ),
+        0,
+    ).astype(BF16)
+    owner = group // 2
+    others = me != owner
+    tail_core_copy = remote(tail_part, tail_core, tail_sems.at[0], tail_sems.at[1], sibling)
+    tail_core_copy.start()
+
+    def tail_copy(slot):
+        return remote(tail_sum, tail_recv.at[slot], tail_sems.at[2], tail_recv_sem.at[slot], of_group(owner))
+
+    def tail_back(peer):
+        return remote(tail_out, tail_out, tail_send_sem.at[peer], tail_sems.at[3], of_group(peer))
 
     def w_copy(wave, slot, peer):
         return remote(
@@ -453,25 +484,36 @@
         core_copy(wave).wait_recv()
         w_sum[wave][...] = (w_part[wave][qi].astype(F32) + w_core[wave][...].astype(F32)).astype(BF16)
         each(group, lambda i: w_copy(wave, me, lax.rem(me + i, group)).start())
-    tail_next(0)
+    tail_core_copy.wait_recv()
+    tail_sum[...] = (tail_part[...].astype(F32) + tail_core[...].astype(F32)).astype(BF16)
+
+    @pl.when(others)
+    def _():
+        tail_copy(me).start()
 
     for start in starts:
         at = slice(start, start + chunk)
         inputs_grad = norm_backward(post_normed[at] * gain_first, pre_normed[at], inverses[at, 0:1])
         pair_out[at] = (post_scaled[at] + inputs_grad).astype(BF16)
 
-    total = query_part[kj].astype(F32)
-
-    def query_add(i, total):
+    def query_wait(i):
         peer = lax.rem(kj + n_kj - i, n_kj)
         query_copy(peer, peer).wait_recv()
-        return total + query_recv[peer].astype(F32)
-
-    query_out[...] = lax.fori_loop(1, n_kj, query_add, total).astype(BF16)
-    kv_copy.wait_recv()
-    kv_total = kv_part[qi].astype(F32) + kv_recv[...].astype(F32)
-    key_out[...] = kv_total[:, :width].astype(BF16)
-    value_out[...] = kv_total[:, width:].astype(BF16)
+
+    def kv_wait(i):
+        peer = lax.rem(cell + n_qi * n_kj - i, n_qi * n_kj)
+        kv_copy(peer, peer).wait_recv()
+
+    each(n_kj, query_wait)
+    each(n_qi * n_kj, kv_wait)
+    for j in range(n_kj):
+        at = slice(j * part, (j + 1) * part)
+        query_out[:, at] = query_recv[j]
+        for out, which in ((key_out, 0), (value_out, 1)):
+            total = kv_recv[j, which].astype(F32)
+            for i in range(1, n_qi):
+                total += kv_recv[i * n_kj + j, which].astype(F32)
+            out[:, at] = total.astype(BF16)
 
     for wave in range(waves):
 
@@ -483,8 +525,17 @@
         total = lax.fori_loop(1, group, w_add, w_sum[wave][me].astype(F32))
         weight_out[wave][qi, me] = (total * (1.0 / (rows * n_qi))).astype(BF16)
         each(group, lambda i: all_copy(wave, me, lax.rem(me + i, group)).start())
-        if 1 + wave < tail_steps:
-            tail_next(1 + wave)
+
+    @pl.when(jnp.logical_not(others))
+    def _():
+        def tail_add(i, total):
+            peer = lax.rem(me + group - i, group)
+            tail_copy(peer).wait_recv()
+            return total + tail_recv[peer].astype(F32)
+
+        total = lax.fori_loop(1, group, tail_add, tail_sum[...].astype(F32))
+        tail_out[...] = (total * (1.0 / (rows * n_qi))).astype(BF16)
+        each(group, lambda i: tail_back(lax.rem(me + i, group)).start())
 
     for wave in range(waves):
 
@@ -494,11 +545,15 @@
 
         each(group, all_wait)
         fwd_copy(wave, qi).start()
-        if 1 + waves + wave < tail_steps:
-            tail_next(1 + waves + wave)
-    for step in range(1 + 2 * waves, tail_steps):
-        tail_next(step)
-    tail_out[...] = tail_own[tail_steps] * (1.0 / (rows * n_qi))
+
+    @pl.when(others)
+    def _():
+        tail_back(me).wait_recv()
+        tail_copy(me).wait_send()
+
+    @pl.when(jnp.logical_not(others))
+    def _():
+        each(group, lambda i: tail_back(lax.rem(me + i, group)).wait_send())
 
     for wave in range(waves):
         fwd_copy(wave, 1 - qi).wait_recv()
@@ -511,23 +566,22 @@
 
         each(group, drain)
         core_copy(wave).wait_send()
-    for step in range(tail_steps):
-        tail_copy(step).wait_send()
-
-    def drain_noise(i):
-        peer = lax.rem(noise + i, n_noise)
-        bias_copy(noise, peer).wait_send()
-        grad_copy(noise, peer).wait_send()
-
-    each(n_noise, drain_noise)
+    tail_core_copy.wait_send()
+
+    def drain_group(i):
+        peer = lax.rem(me + i, group)
+        bias_copy(me, peer).wait_send()
+        grad_copy(me, peer).wait_send()
+
+    each(group, drain_group)
 
     def drain_kj(i):
         peer = lax.rem(kj + i, n_kj)
-        stat_copy(kj, peer).wait_send()
+        tile_copy(kj, peer).wait_send()
         query_copy(kj, peer).wait_send()
 
     each(n_kj, drain_kj)
-    kv_copy.wait_send()
+    each(n_qi * n_kj, lambda i: kv_copy(cell, lax.rem(cell + i, n_qi * n_kj)).wait_send())
 
 
 def finish(
@@ -552,6 +606,7 @@
     gate_wide,
     up_wide,
     down_wide,
+    head_wide,
     first_wide,
     second_wide,
     sems,
@@ -588,9 +643,11 @@
     for t in range(tiles):
         up_wide[:, t * channels : (t + 1) * channels] = tile(2 * tiles + t)
     store(up_wide, up_out)
-    store(tail_ref.at[pl.ds(0, HEADS)], head_out)
-    first_wide[...] = tail_ref[HEADS : HEADS + 1]
-    second_wide[...] = tail_ref[HEADS + 1 : HEADS + 2]
+    tail = tail_ref[...].astype(F32)
+    head_wide[...] = tail[0:HEADS]
+    store(head_wide, head_out)
+    first_wide[...] = tail[HEADS : HEADS + 1]
+    second_wide[...] = tail[HEADS + ALIGN // 2 : HEADS + ALIGN // 2 + 1]
     store(first_wide, first_out)
     store(second_wide, second_out)
     for copy in copies:
@@ -628,11 +685,12 @@
         (n_qi, group, -(-part // (BLOCK * devices)) * BLOCK, channels) for part in parts_of
     )
     tail_shape = (HEADS + ALIGN, channels)
-    tail_steps = 1 + (group - 1).bit_length()
     half = keys // n_qi
     q_half = rows // n_kj
     sizes = (n_noise, n_qi, n_kj, rows, keys, share, parts_of)
-    pack = max(1, LANES // keys)
+    own = HEADS // n_kj
+    part = own * HEAD_DIM
+    pack = min(own, max(1, LANES // keys))
     vmem = pl.BlockSpec(memory_space=pltpu.VMEM)
     dma = pltpu.SemaphoreType.DMA
 
@@ -660,38 +718,53 @@
         pltpu.VMEM((count, channels), BF16),
         pltpu.VMEM((count, 128), F32),
         pltpu.VMEM((share, HEADS, keys), F32),
-        pltpu.VMEM((n_noise, HEADS // pack, share, pack * keys), BF16),
-        pltpu.VMEM((HEADS, rows, keys), F32),
-        pltpu.VMEM((HEADS, rows, keys), F32),
-        pltpu.VMEM((n_kj, rows, 128), F32),
-        pltpu.VMEM((n_noise, HEADS // pack, share, pack * keys), BF16),
-        pltpu.VMEM((n_noise, HEADS // pack, share, pack * keys), BF16),
-        pltpu.VMEM((HEADS // pack, share, pack * keys), F32),
+        pltpu.VMEM((n_kj, own // pack, share, pack * keys), BF16),
+        pltpu.VMEM((group, own // pack, share, pack * keys), BF16),
+        pltpu.VMEM((n_kj, rows, part), BF16),
+        pltpu.VMEM((n_kj, rows, part), BF16),
+        pltpu.VMEM((n_kj, 2, keys, part), BF16),
+        pltpu.VMEM((n_kj, 2, keys, part), BF16),
+        pltpu.VMEM((own * rows, part), BF16),
+        pltpu.VMEM((own * rows, part), BF16),
+        pltpu.VMEM((own * n_kj * keys, part), BF16),
+        pltpu.VMEM((own * rows, n_kj * keys), F32),
+        pltpu.VMEM((own * rows, n_kj * keys), F32),
+        pltpu.VMEM((own * rows, n_kj * keys), BF16),
+        pltpu.VMEM((own * rows, n_kj * keys), BF16),
+        pltpu.VMEM((rows, own * n_kj * keys), BF16),
+        pltpu.VMEM((group, own // pack, share, pack * keys), BF16),
+        pltpu.VMEM((group, own // pack, share, pack * keys), BF16),
+        pltpu.VMEM((n_kj, own // pack, share, pack * keys), F32),
         pltpu.VMEM((count, channels), F32),
-        pltpu.VMEM((n_kj, q_half, width), BF16),
-        pltpu.VMEM((n_kj, q_half, width), BF16),
-        pltpu.VMEM((n_qi, half, 2 * width), BF16),
-        pltpu.VMEM((half, 2 * width), BF16),
-        pltpu.VMEM((1 + tail_steps, *tail_shape), F32),
-        pltpu.VMEM((tail_steps, *tail_shape), F32),
+        pltpu.VMEM((n_kj, q_half, part), BF16),
+        pltpu.VMEM((n_kj, q_half, part), BF16),
+        pltpu.VMEM((n_qi * n_kj, 2, half, part), BF16),
+        pltpu.VMEM((n_qi * n_kj, 2, half, part), BF16),
+        pltpu.VMEM(tail_shape, BF16),
+        pltpu.VMEM(tail_shape, BF16),
+        pltpu.VMEM(tail_shape, BF16),
+        pltpu.VMEM((group, *tail_shape), BF16),
         dma((11,)),
-        dma((n_noise,)),
-        dma((n_noise,)),
+        dma((group,)),
+        dma((group,)),
         dma((n_kj,)),
         dma((n_kj,)),
-        dma((n_noise,)),
-        dma((n_noise,)),
+        dma((group,)),
+        dma((group,)),
         dma((n_kj,)),
         dma((n_kj,)),
-        dma((6,)),
+        dma((n_qi * n_kj,)),
+        dma((n_qi * n_kj,)),
+        dma((2 * len(waves),)),
         dma((len(waves) * group,)),
         dma((len(waves) * group,)),
         dma((len(waves) * group,)),
         dma((len(waves) * group,)),
         dma((len(waves),)),
         dma((len(waves),)),
-        dma((tail_steps,)),
-        dma((tail_steps,)),
+        dma((4,)),
+        dma((group,)),
+        dma((group,)),
     ]
     wave_scratch = [
         [pltpu.VMEM(wave[skip:], BF16) for wave in waves] for skip in (0, 1, 1, 1)
@@ -716,7 +789,7 @@
             jax.ShapeDtypeStruct((half, width), BF16),
             jax.ShapeDtypeStruct((half, width), BF16),
             jax.ShapeDtypeStruct((count, channels), BF16),
-            jax.ShapeDtypeStruct(tail_shape, F32),
+            jax.ShapeDtypeStruct(tail_shape, BF16),
             *(jax.ShapeDtypeStruct(wave, BF16) for wave in waves),
         ),
         in_specs=[hbm] * 11,
@@ -767,6 +840,7 @@
             pltpu.VMEM((channels, hidden_count), F32),
             pltpu.VMEM((channels, hidden_count), F32),
             pltpu.VMEM((hidden_count, channels), F32),
+            pltpu.VMEM((HEADS, channels), F32),
             pltpu.VMEM((1, channels), F32),
             pltpu.VMEM((1, channels), F32),
             dma((10,)),

time: 42.9 us -> 38.4 us (0.90)
  Pallas kernels: 42.1 us -> 37.5 us
    pallas_call x1, Pallas kernels: 41 us -> 36.5 us  [local(): pl.pallas_call(run, out_shape=(jax.ShapeDtypeStruct((q_half, width), BF16...]
where the time goes in v2:
time: 38.4 us; the launch traced here: 38.2 us
  Pallas kernels  37.5 us (98%)
  between operations  0.65 us (2%)
    pallas_call x1, Pallas kernels, local(): pl.pallas_call(run, out_shape=(jax.ShapeDtypeStruct((q_half, width), BF16...  36.5 us
    pallas_call x1, Pallas kernels, local(): pl.pallas_call(finish_all, out_shape=tuple((jax.ShapeDtypeStruct(x.shape,...  1.07 us

profile of v2, /device:TPU:0, one launch (start us, length us, event | category | flops | bytes accessed | tf_op | source)
XLA Modules:
  0.0 38.2 jit_solution(1392741755801940898)
XLA Ops:
  0.6 36.5 %block_backward.1 = (bf16[32,768]{1,0:T(8,128)(2,1)S(1)}, bf16[32,768]{1,0:T(8,128)(2,1)S(1)}, bf16[32,768]{1,0:T(8,128)(2,1)S(1)}, bf16[512,128]{1,0:T(8,128)(2...) custom-call(bf16[64,2,32,128]{3,2,1,0:T(8,128)(2,1)} %refs_0_.1, ...), custom_call_target="tpu_custom_call" | custom-call | tf_op jit(solution)/shard_map/block_backward/pallas_call | solution.py:785
  37.1 1.1 %finish_weights.1 = (bf16[32,768]{1,0:T(8,128)(2,1)}, bf16[32,768]{1,0:T(8,128)(2,1)}, bf16[32,768]{1,0:T(8,128)(2,1)}, bf16[512,128]{1,0:T(8,128)(2,1)}, f32[12...) custom-call(bf16[24,128]{1,0:T(8,128)(2,1)S(1)} %get-tuple-element.2, ...), custom_call_target="tpu_custom_call" | custom-call | tf_op jit(solution)/shard_map/finish_weights/pallas_call | solution.py:826

commit v3 on v2

--- a/solution.py
+++ b/solution.py
@@ -150,6 +150,7 @@
     qi = lax.axis_index("qi")
     kj = lax.axis_index("kj")
     me = noise * n_kj + kj
+    power = group & (group - 1) == 0
     sibling = {"qi": 1 - qi}
     channels = cells.shape[-1]
     width = q_ref.shape[-1]
@@ -170,6 +171,12 @@
 
     def of_group(index):
         return {"noise": index // n_kj, "kj": lax.rem(index, n_kj)}
+
+    def far(i):
+        return lax.bitwise_xor(me, group - i) if power else lax.rem(me + i, group)
+
+    def near(i):
+        return lax.bitwise_xor(me, i) if power else lax.rem(me + group - i, group)
 
     def each(count, body):
         def step(i, carry):
@@ -203,7 +210,7 @@
 
     def greet(i):
         pl.semaphore_signal(
-            barrier, inc=1, device_id=of_group(lax.rem(me + i, group)), device_id_type=MESH
+            barrier, inc=1, device_id=of_group(far(i)), device_id_type=MESH
         )
 
     each(group, greet)
@@ -271,7 +278,7 @@
         )
 
     each(n_kj, lambda i: tile_copy(kj, lax.rem(kj + i, n_kj)).start())
-    each(group, lambda i: bias_copy(me, lax.rem(me + i, group)).start())
+    each(group, lambda i: bias_copy(me, far(i)).start())
 
     kv_all[kj] = kv_send[kj]
     bias_all[me] = bias_send[kj]
@@ -306,7 +313,7 @@
         k_heads[h * n_kj * keys : (h + 1) * n_kj * keys] = k_own * mask(h)
 
     def bias_wait(i):
-        peer = lax.rem(me + group - i, group)
+        peer = near(i)
         bias_copy(peer, peer).wait_recv()
 
     each(group, bias_wait)
@@ -337,7 +344,7 @@
             grad_send.at[peer], grad_recv.at[slot], grad_send_sem.at[peer], grad_recv_sem.at[slot], of_group(peer)
         )
 
-    each(group, lambda i: grad_copy(me, lax.rem(me + i, group)).start())
+    each(group, lambda i: grad_copy(me, far(i)).start())
 
     query_all = (dot(score_cat[...], k_heads[...], 1, 0) * scale).astype(BF16)
     for j in range(n_kj):
@@ -368,7 +375,7 @@
     grad_recv[me] = grad_send[me]
 
     def grad_wait(i):
-        peer = lax.rem(me + group - i, group)
+        peer = near(i)
         grad_copy(peer, peer).wait_recv()
 
     each(group, grad_wait)
@@ -483,7 +490,7 @@
     for wave in range(waves):
         core_copy(wave).wait_recv()
         w_sum[wave][...] = (w_part[wave][qi].astype(F32) + w_core[wave][...].astype(F32)).astype(BF16)
-        each(group, lambda i: w_copy(wave, me, lax.rem(me + i, group)).start())
+        each(group, lambda i: w_copy(wave, me, far(i)).start())
     tail_core_copy.wait_recv()
     tail_sum[...] = (tail_part[...].astype(F32) + tail_core[...].astype(F32)).astype(BF16)
 
@@ -518,29 +525,29 @@
     for wave in range(waves):
 
         def w_add(i, total):
-            peer = lax.rem(me + group - i, group)
+            peer = near(i)
             w_copy(wave, peer, peer).wait_recv()
             return total + w_recv[wave][peer].astype(F32)
 
         total = lax.fori_loop(1, group, w_add, w_sum[wave][me].astype(F32))
         weight_out[wave][qi, me] = (total * (1.0 / (rows * n_qi))).astype(BF16)
-        each(group, lambda i: all_copy(wave, me, lax.rem(me + i, group)).start())
+        each(group, lambda i: all_copy(wave, me, far(i)).start())
 
     @pl.when(jnp.logical_not(others))
     def _():
         def tail_add(i, total):
-            peer = lax.rem(me + group - i, group)
+            peer = near(i)
             tail_copy(peer).wait_recv()
             return total + tail_recv[peer].astype(F32)
 
         total = lax.fori_loop(1, group, tail_add, tail_sum[...].astype(F32))
         tail_out[...] = (total * (1.0 / (rows * n_qi))).astype(BF16)
-        each(group, lambda i: tail_back(lax.rem(me + i, group)).start())
+        each(group, lambda i: tail_back(far(i)).start())
 
     for wave in range(waves):
 
         def all_wait(i):
-            peer = lax.rem(me + group - i, group)
+            peer = near(i)
             all_copy(wave, peer, peer).wait_recv()
 
         each(group, all_wait)
@@ -553,14 +560,14 @@
 
     @pl.when(jnp.logical_not(others))
     def _():
-        each(group, lambda i: tail_back(lax.rem(me + i, group)).wait_send())
+        each(group, lambda i: tail_back(far(i)).wait_send())
 
     for wave in range(waves):
         fwd_copy(wave, 1 - qi).wait_recv()
         fwd_copy(wave, qi).wait_send()
 
         def drain(i):
-            peer = lax.rem(me + i, group)
+            peer = far(i)
             w_copy(wave, me, peer).wait_send()
             all_copy(wave, me, peer).wait_send()
 
@@ -569,7 +576,7 @@
     tail_core_copy.wait_send()
 
     def drain_group(i):
-        peer = lax.rem(me + i, group)
+        peer = far(i)
         bias_copy(me, peer).wait_send()
         grad_copy(me, peer).wait_send()
 

time: 38.4 us -> 37.1 us (0.966)
  Pallas kernels: 37.5 us -> 36.3 us
    pallas_call x1, Pallas kernels: 36.5 us -> 35.3 us  [local(): pl.pallas_call(run, out_shape=(jax.ShapeDtypeStruct((q_half, width), BF16...]
where the time goes in v3:
time: 37.1 us; the launch traced here: 37 us
  Pallas kernels  36.3 us (98%)
  between operations  0.65 us (2%)
    pallas_call x1, Pallas kernels, local(): pl.pallas_call(run, out_shape=(jax.ShapeDtypeStruct((q_half, width), BF16...  35.3 us
    pallas_call x1, Pallas kernels, local(): pl.pallas_call(finish_all, out_shape=tuple((jax.ShapeDtypeStruct(x.shape,...  1.07 us

profile of v3, /device:TPU:0, one launch (start us, length us, event | category | flops | bytes accessed | tf_op | source)
XLA Modules:
  0.0 37.0 jit_solution(12680451151121857229)
XLA Ops:
  0.6 35.3 %block_backward.1 = (bf16[32,768]{1,0:T(8,128)(2,1)S(1)}, bf16[32,768]{1,0:T(8,128)(2,1)S(1)}, bf16[32,768]{1,0:T(8,128)(2,1)S(1)}, bf16[512,128]{1,0:T(8,128)(2...) custom-call(bf16[64,2,32,128]{3,2,1,0:T(8,128)(2,1)} %refs_0_.1, ...), custom_call_target="tpu_custom_call" | custom-call | tf_op jit(solution)/shard_map/block_backward/pallas_call | solution.py:792
  35.9 1.1 %finish_weights.1 = (bf16[32,768]{1,0:T(8,128)(2,1)}, bf16[32,768]{1,0:T(8,128)(2,1)}, bf16[32,768]{1,0:T(8,128)(2,1)}, bf16[512,128]{1,0:T(8,128)(2,1)}, f32[12...) custom-call(bf16[24,128]{1,0:T(8,128)(2,1)S(1)} %get-tuple-element.2, ...), custom_call_target="tpu_custom_call" | custom-call | tf_op jit(solution)/shard_map/finish_weights/pallas_call | solution.py:833

commit v4 on v2

--- a/solution.py
+++ b/solution.py
@@ -12,6 +12,7 @@
 HEAD_DIM = 48
 ALIGN = 8
 BLOCK = 16
+UNROLLED = 16
 LANES = 128
 
 epsilon = 1e-05
@@ -114,26 +115,20 @@
     tail_sum,
     tail_recv,
     input_sems,
-    bias_send_sem,
-    bias_recv_sem,
+    bias_sems,
     tile_send_sem,
     tile_recv_sem,
-    grad_send_sem,
-    grad_recv_sem,
+    grad_sems,
     query_send_sem,
     query_recv_sem,
     kv_send_sem,
     kv_recv_sem,
     pair_sems,
-    w_send_sem,
-    w_recv_sem,
-    all_send_sem,
-    all_recv_sem,
+    w_sems,
+    all_sems,
     fwd_send_sem,
     fwd_recv_sem,
     tail_sems,
-    tail_send_sem,
-    tail_recv_sem,
     weight_out,
     w_part,
     w_core,
@@ -168,15 +163,38 @@
             src_ref=src, dst_ref=dst, send_sem=send, recv_sem=recv, device_id=device, device_id_type=MESH
         )
 
-    def of_group(index):
-        return {"noise": index // n_kj, "kj": lax.rem(index, n_kj)}
+    def away(offset):
+        if isinstance(offset, int):
+            steps = (offset // n_kj, offset % n_kj)
+            return {
+                name: lax.bitwise_xor(at, step) for name, at, step in zip(("noise", "kj"), (noise, kj), steps) if step
+            }
+        return {
+            "noise": lax.bitwise_xor(noise, lax.div(offset, n_kj)),
+            "kj": lax.bitwise_xor(kj, lax.rem(offset, n_kj)),
+        }
 
     def each(count, body):
+        if count <= UNROLLED:
+            for i in range(1, count):
+                body(i)
+            return
+
         def step(i, carry):
             body(i)
             return carry
 
         lax.fori_loop(1, count, step, 0)
+
+    def added(count, total, term):
+        if count <= UNROLLED:
+            for i in range(1, count):
+                total += term(i)
+            return total
+        return lax.fori_loop(1, count, lambda i, total: total + term(i), total)
+
+    def moved(view, sems):
+        return remote(view, view, sems.at[0], sems.at[1], sibling)
 
     forward_loads = [
         pltpu.make_async_copy(src, dst, input_sems.at[i])
@@ -201,13 +219,11 @@
 
     barrier = pltpu.get_barrier_semaphore()
 
-    def greet(i):
-        pl.semaphore_signal(
-            barrier, inc=1, device_id=of_group(lax.rem(me + i, group)), device_id_type=MESH
-        )
-
-    each(group, greet)
-    pl.semaphore_signal(barrier, inc=1, device_id=sibling, device_id_type=MESH)
+    def greet(device):
+        pl.semaphore_signal(barrier, inc=1, device_id=device, device_id_type=MESH)
+
+    each(group, lambda i: greet(away(group - i)))
+    greet(sibling)
     for load in attention_loads:
         load.start()
     for load in forward_loads:
@@ -256,22 +272,26 @@
 
     pl.semaphore_wait(barrier, group)
 
-    def tile_copy(slot, peer):
+    def tile_copy(offset):
         return remote(
-            kv_send.at[peer], kv_all.at[slot], tile_send_sem.at[peer], tile_recv_sem.at[slot], {"kj": peer}
-        )
-
-    def bias_copy(slot, peer):
+            kv_send.at[lax.bitwise_xor(kj, offset)],
+            kv_all.at[kj],
+            tile_send_sem.at[offset],
+            tile_recv_sem.at[offset],
+            {"kj": lax.bitwise_xor(kj, offset)},
+        )
+
+    def bias_copy(offset):
         return remote(
-            bias_send.at[lax.rem(peer, n_kj)],
-            bias_all.at[slot],
-            bias_send_sem.at[peer],
-            bias_recv_sem.at[slot],
-            of_group(peer),
-        )
-
-    each(n_kj, lambda i: tile_copy(kj, lax.rem(kj + i, n_kj)).start())
-    each(group, lambda i: bias_copy(me, lax.rem(me + i, group)).start())
+            bias_send.at[lax.bitwise_xor(kj, lax.rem(offset, n_kj))],
+            bias_all.at[me],
+            bias_sems.at[0],
+            bias_sems.at[1],
+            away(offset),
+        )
+
+    each(n_kj, lambda i: tile_copy(i).start())
+    each(group, lambda i: bias_copy(group - i).start())
 
     kv_all[kj] = kv_send[kj]
     bias_all[me] = bias_send[kj]
@@ -293,11 +313,7 @@
         if count < math.prod(w_part[wave].shape[:3]):
             w_part[wave][...] = jnp.zeros(w_part[wave].shape, BF16)
 
-    def tile_wait(i):
-        peer = lax.rem(kj + n_kj - i, n_kj)
-        tile_copy(peer, peer).wait_recv()
-
-    each(n_kj, tile_wait)
+    each(n_kj, lambda i: tile_copy(i).wait_recv())
     k_own = kv_all[:, 0].reshape(n_kj * keys, part)
     v_own = kv_all[:, 1].reshape(n_kj * keys, part)
     score[...] = dot(q_heads[...], k_own, 1, 1) * scale
@@ -305,11 +321,8 @@
     for h in range(own):
         k_heads[h * n_kj * keys : (h + 1) * n_kj * keys] = k_own * mask(h)
 
-    def bias_wait(i):
-        peer = lax.rem(me + group - i, group)
-        bias_copy(peer, peer).wait_recv()
-
-    each(group, bias_wait)
+    others = pl.ds(1, group - 1)
+    moved(bias_all.at[others], bias_sems).wait_recv()
 
     for p in range(packed):
         blocks = [
@@ -332,12 +345,16 @@
             for n in range(n_noise):
                 grad_send[n * n_kj + j, p] = piece[n * share : (n + 1) * share]
 
-    def grad_copy(slot, peer):
+    def grad_copy(offset):
         return remote(
-            grad_send.at[peer], grad_recv.at[slot], grad_send_sem.at[peer], grad_recv_sem.at[slot], of_group(peer)
-        )
-
-    each(group, lambda i: grad_copy(me, lax.rem(me + i, group)).start())
+            grad_send.at[lax.bitwise_xor(me, offset)],
+            grad_recv.at[offset],
+            grad_sems.at[0],
+            grad_sems.at[1],
+            away(offset),
+        )
+
+    each(group, lambda i: grad_copy(group - i).start())
 
     query_all = (dot(score_cat[...], k_heads[...], 1, 0) * scale).astype(BF16)
     for j in range(n_kj):
@@ -350,33 +367,44 @@
             kv_part[i * n_kj + j, 0] = key_all[at]
             kv_part[i * n_kj + j, 1] = value_all[at]
 
-    def query_copy(slot, peer):
+    def query_copy(offset):
         return remote(
-            query_part.at[peer], query_recv.at[slot], query_send_sem.at[peer], query_recv_sem.at[slot], {"kj": peer}
-        )
-
-    def kv_copy(slot, peer):
-        device = {"qi": peer // n_kj, "kj": lax.rem(peer, n_kj)}
-        return remote(kv_part.at[peer], kv_recv.at[slot], kv_send_sem.at[peer], kv_recv_sem.at[slot], device)
+            query_part.at[lax.bitwise_xor(kj, offset)],
+            query_recv.at[kj],
+            query_send_sem.at[offset],
+            query_recv_sem.at[offset],
+            {"kj": lax.bitwise_xor(kj, offset)},
+        )
 
     cell = qi * n_kj + kj
-    each(n_kj, lambda i: query_copy(kj, lax.rem(kj + i, n_kj)).start())
-    each(n_qi * n_kj, lambda i: kv_copy(cell, lax.rem(cell + i, n_qi * n_kj)).start())
+
+    def kv_copy(offset):
+        if isinstance(offset, int):
+            steps = (offset // n_kj, offset % n_kj)
+        else:
+            steps = (lax.div(offset, n_kj), lax.rem(offset, n_kj))
+        return remote(
+            kv_part.at[lax.bitwise_xor(cell, offset)],
+            kv_recv.at[cell],
+            kv_send_sem.at[offset],
+            kv_recv_sem.at[offset],
+            {"qi": lax.bitwise_xor(qi, steps[0]), "kj": lax.bitwise_xor(kj, steps[1])},
+        )
+
+    each(n_kj, lambda i: query_copy(i).start())
+    each(n_qi * n_kj, lambda i: kv_copy(i).start())
     query_recv[kj] = query_part[kj]
     kv_recv[cell] = kv_part[cell]
-
-    grad_recv[me] = grad_send[me]
-
-    def grad_wait(i):
-        peer = lax.rem(me + group - i, group)
-        grad_copy(peer, peer).wait_recv()
-
-    each(group, grad_wait)
+    each(n_kj, lambda i: tile_copy(i).wait_send())
+    moved(bias_all.at[others], bias_sems).wait_send()
+
+    grad_recv[0] = grad_send[me]
+    moved(grad_recv.at[others], grad_sems).wait_recv()
     for j in range(n_kj):
         total = grad_recv[j].astype(F32)
-        for n in range(1, n_noise):
-            total += grad_recv[n * n_kj + j].astype(F32)
-        grad_sum[j] = total
+        grad_sum[lax.bitwise_xor(kj, j)] = added(
+            n_noise, total, lambda n: grad_recv[n * n_kj + j].astype(F32)
+        )
 
     head_part = jnp.zeros((HEADS, channels), F32)
     for i in range(share):
@@ -451,61 +479,55 @@
         0,
     ).astype(BF16)
     owner = group // 2
-    others = me != owner
+    to_owner = lax.bitwise_xor(me, owner)
     tail_core_copy = remote(tail_part, tail_core, tail_sems.at[0], tail_sems.at[1], sibling)
     tail_core_copy.start()
 
-    def tail_copy(slot):
-        return remote(tail_sum, tail_recv.at[slot], tail_sems.at[2], tail_recv_sem.at[slot], of_group(owner))
-
-    def tail_back(peer):
-        return remote(tail_out, tail_out, tail_send_sem.at[peer], tail_sems.at[3], of_group(peer))
-
-    def w_copy(wave, slot, peer):
+    def tail_copy():
+        device = {"noise": owner // n_kj, "kj": owner % n_kj}
+        return remote(tail_sum, tail_recv.at[to_owner], tail_sems.at[2], tail_sems.at[3], device)
+
+    def tail_back(offset):
+        return remote(tail_out, tail_out, tail_sems.at[4], tail_sems.at[5], away(offset))
+
+    def w_copy(wave, offset):
         return remote(
-            w_sum[wave].at[peer],
-            w_recv[wave].at[slot],
-            w_send_sem.at[wave * group + peer],
-            w_recv_sem.at[wave * group + slot],
-            of_group(peer),
-        )
-
-    def all_copy(wave, slot, peer):
-        at = weight_out[wave].at[qi, slot]
-        return remote(
-            at, at, all_send_sem.at[wave * group + peer], all_recv_sem.at[wave * group + slot], of_group(peer)
-        )
+            w_sum[wave].at[lax.bitwise_xor(me, offset)],
+            w_recv[wave].at[offset],
+            w_sems.at[2 * wave],
+            w_sems.at[2 * wave + 1],
+            away(offset),
+        )
+
+    def all_copy(wave, offset):
+        at = weight_out[wave].at[qi, me]
+        return remote(at, at, all_sems.at[2 * wave], all_sems.at[2 * wave + 1], away(offset))
 
     def fwd_copy(wave, core):
         at = weight_out[wave].at[core]
         return remote(at, at, fwd_send_sem.at[wave], fwd_recv_sem.at[wave], sibling)
 
+    def pair_of(sems, wave):
+        return sems.at[pl.ds(2 * wave, 2)]
+
     for wave in range(waves):
         core_copy(wave).wait_recv()
         w_sum[wave][...] = (w_part[wave][qi].astype(F32) + w_core[wave][...].astype(F32)).astype(BF16)
-        each(group, lambda i: w_copy(wave, me, lax.rem(me + i, group)).start())
+        each(group, lambda i: w_copy(wave, group - i).start())
     tail_core_copy.wait_recv()
     tail_sum[...] = (tail_part[...].astype(F32) + tail_core[...].astype(F32)).astype(BF16)
 
-    @pl.when(others)
+    @pl.when(to_owner != 0)
     def _():
-        tail_copy(me).start()
+        tail_copy().start()
 
     for start in starts:
         at = slice(start, start + chunk)
         inputs_grad = norm_backward(post_normed[at] * gain_first, pre_normed[at], inverses[at, 0:1])
         pair_out[at] = (post_scaled[at] + inputs_grad).astype(BF16)
 
-    def query_wait(i):
-        peer = lax.rem(kj + n_kj - i, n_kj)
-        query_copy(peer, peer).wait_recv()
-
-    def kv_wait(i):
-        peer = lax.rem(cell + n_qi * n_kj - i, n_qi * n_kj)
-        kv_copy(peer, peer).wait_recv()
-
-    each(n_kj, query_wait)
-    each(n_qi * n_kj, kv_wait)
+    each(n_kj, lambda i: query_copy(i).wait_recv())
+    each(n_qi * n_kj, lambda i: kv_copy(i).wait_recv())
     for j in range(n_kj):
         at = slice(j * part, (j + 1) * part)
         query_out[:, at] = query_recv[j]
@@ -515,73 +537,46 @@
                 total += kv_recv[i * n_kj + j, which].astype(F32)
             out[:, at] = total.astype(BF16)
 
+    each(n_kj, lambda i: query_copy(i).wait_send())
+    each(n_qi * n_kj, lambda i: kv_copy(i).wait_send())
+    moved(grad_recv.at[others], grad_sems).wait_send()
     for wave in range(waves):
-
-        def w_add(i, total):
-            peer = lax.rem(me + group - i, group)
-            w_copy(wave, peer, peer).wait_recv()
-            return total + w_recv[wave][peer].astype(F32)
-
-        total = lax.fori_loop(1, group, w_add, w_sum[wave][me].astype(F32))
+        core_copy(wave).wait_send()
+    tail_core_copy.wait_send()
+
+    for wave in range(waves):
+        moved(w_recv[wave].at[others], pair_of(w_sems, wave)).wait_recv()
+        total = added(group, w_sum[wave][me].astype(F32), lambda i: w_recv[wave][i].astype(F32))
         weight_out[wave][qi, me] = (total * (1.0 / (rows * n_qi))).astype(BF16)
-        each(group, lambda i: all_copy(wave, me, lax.rem(me + i, group)).start())
-
-    @pl.when(jnp.logical_not(others))
+        each(group, lambda i: all_copy(wave, group - i).start())
+
+    @pl.when(to_owner == 0)
     def _():
-        def tail_add(i, total):
-            peer = lax.rem(me + group - i, group)
-            tail_copy(peer).wait_recv()
-            return total + tail_recv[peer].astype(F32)
-
-        total = lax.fori_loop(1, group, tail_add, tail_sum[...].astype(F32))
+        moved(tail_recv.at[others], tail_sems.at[pl.ds(2, 2)]).wait_recv()
+        total = added(group, tail_sum[...].astype(F32), lambda i: tail_recv[i].astype(F32))
         tail_out[...] = (total * (1.0 / (rows * n_qi))).astype(BF16)
-        each(group, lambda i: tail_back(lax.rem(me + i, group)).start())
+        each(group, lambda i: tail_back(group - i).start())
 
     for wave in range(waves):
-
-        def all_wait(i):
-            peer = lax.rem(me + group - i, group)
-            all_copy(wave, peer, peer).wait_recv()
-
-        each(group, all_wait)
+        moved(w_recv[wave].at[others], pair_of(w_sems, wave)).wait_send()
+    for wave in range(waves):
+        moved(weight_out[wave].at[qi, others], pair_of(all_sems, wave)).wait_recv()
         fwd_copy(wave, qi).start()
 
-    @pl.when(others)
+    @pl.when(to_owner != 0)
     def _():
-        tail_back(me).wait_recv()
-        tail_copy(me).wait_send()
-
-    @pl.when(jnp.logical_not(others))
+        remote(tail_out, tail_out, tail_sems.at[4], tail_sems.at[5], sibling).wait_recv()
+        tail_copy().wait_send()
+
+    @pl.when(to_owner == 0)
     def _():
-        each(group, lambda i: tail_back(lax.rem(me + i, group)).wait_send())
-
+        moved(tail_recv.at[others], tail_sems.at[pl.ds(4, 2)]).wait_send()
+
+    for wave in range(waves):
+        moved(weight_out[wave].at[qi, others], pair_of(all_sems, wave)).wait_send()
     for wave in range(waves):
         fwd_copy(wave, 1 - qi).wait_recv()
         fwd_copy(wave, qi).wait_send()
-
-        def drain(i):
-            peer = lax.rem(me + i, group)
-            w_copy(wave, me, peer).wait_send()
-            all_copy(wave, me, peer).wait_send()
-
-        each(group, drain)
-        core_copy(wave).wait_send()
-    tail_core_copy.wait_send()
-
-    def drain_group(i):
-        peer = lax.rem(me + i, group)
-        bias_copy(me, peer).wait_send()
-        grad_copy(me, peer).wait_send()
-
-    each(group, drain_group)
-
-    def drain_kj(i):
-        peer = lax.rem(kj + i, n_kj)
-        tile_copy(kj, peer).wait_send()
-        query_copy(kj, peer).wait_send()
-
-    each(n_kj, drain_kj)
-    each(n_qi * n_kj, lambda i: kv_copy(cell, lax.rem(cell + i, n_qi * n_kj)).wait_send())
 
 
 def finish(
@@ -745,26 +740,20 @@
         pltpu.VMEM(tail_shape, BF16),
         pltpu.VMEM((group, *tail_shape), BF16),
         dma((11,)),
-        dma((group,)),
-        dma((group,)),
+        dma((2,)),
         dma((n_kj,)),
         dma((n_kj,)),
-        dma((group,)),
-        dma((group,)),
+        dma((2,)),
         dma((n_kj,)),
         dma((n_kj,)),
         dma((n_qi * n_kj,)),
         dma((n_qi * n_kj,)),
         dma((2 * len(waves),)),
-        dma((len(waves) * group,)),
-        dma((len(waves) * group,)),
-        dma((len(waves) * group,)),
-        dma((len(waves) * group,)),
+        dma((2 * len(waves),)),
+        dma((2 * len(waves),)),
         dma((len(waves),)),
         dma((len(waves),)),
-        dma((4,)),
-        dma((group,)),
-        dma((group,)),
+        dma((6,)),
     ]
     wave_scratch = [
         [pltpu.VMEM(wave[skip:], BF16) for wave in waves] for skip in (0, 1, 1, 1)

time: 38.4 us -> 34.5 us (0.90)
  Pallas kernels: 37.5 us -> 33.7 us
    pallas_call x1, Pallas kernels: 36.5 us -> 32.6 us  [local(): pl.pallas_call(run, out_shape=(jax.ShapeDtypeStruct((q_half, width), BF16...]
where the time goes in v4:
time: 34.5 us; the launch traced here: 34.4 us
  Pallas kernels  33.7 us (98%)
  between operations  0.65 us (2%)
    pallas_call x1, Pallas kernels, local(): pl.pallas_call(run, out_shape=(jax.ShapeDtypeStruct((q_half, width), BF16...  32.6 us
    pallas_call x1, Pallas kernels, local(): pl.pallas_call(finish_all, out_shape=tuple((jax.ShapeDtypeStruct(x.shape,...  1.07 us

profile of v4, /device:TPU:0, one launch (start us, length us, event | category | flops | bytes accessed | tf_op | source)
XLA Modules:
  0.0 34.4 jit_solution(8611330468818730738)
XLA Ops:
  0.6 32.6 %block_backward.1 = (bf16[32,768]{1,0:T(8,128)(2,1)S(1)}, bf16[32,768]{1,0:T(8,128)(2,1)S(1)}, bf16[32,768]{1,0:T(8,128)(2,1)S(1)}, bf16[512,128]{1,0:T(8,128)(2...) custom-call(bf16[64,2,32,128]{3,2,1,0:T(8,128)(2,1)} %refs_0_.1, ...), custom_call_target="tpu_custom_call" | custom-call | tf_op jit(solution)/shard_map/block_backward/pallas_call | solution.py:774
  33.3 1.1 %finish_weights.1 = (bf16[32,768]{1,0:T(8,128)(2,1)}, bf16[32,768]{1,0:T(8,128)(2,1)}, bf16[32,768]{1,0:T(8,128)(2,1)}, bf16[512,128]{1,0:T(8,128)(2,1)}, f32[12...) custom-call(bf16[24,128]{1,0:T(8,128)(2,1)S(1)} %get-tuple-element.2, ...), custom_call_target="tpu_custom_call" | custom-call | tf_op jit(solution)/shard_map/finish_weights/pallas_call | solution.py:815

commit v5 on v4

--- a/solution.py
+++ b/solution.py
@@ -84,6 +84,7 @@
     hidden,
     hidden_t,
     up_low,
+    updated_low,
     post_normed,
     post_low,
     inverses,
@@ -333,9 +334,11 @@
             at = slice(h * rows, (h + 1) * rows)
             full = score[at] + jnp.concatenate([block[:, i * keys : (i + 1) * keys] for block in blocks], 1)
             expo = jnp.exp(full - jnp.max(full, axis=1, keepdims=True))
-            attend = expo * (1.0 / jnp.sum(expo, axis=1, keepdims=True))
             weighed = attend_grad[at]
-            score_grad = attend * (weighed - jnp.sum(attend * weighed, axis=1, keepdims=True))
+            inverse = 1.0 / jnp.sum(expo, axis=1, keepdims=True)
+            delta = jnp.sum(expo * weighed, axis=1, keepdims=True) * inverse
+            attend = expo * inverse
+            score_grad = attend * (weighed - delta)
             grads.append(score_grad)
             attend_low[at] = attend.astype(BF16)
             score_low[at] = score_grad.astype(BF16)
@@ -426,49 +429,71 @@
             count, block, channels
         )
 
+    def core_copy(wave):
+        return remote(
+            w_part[wave].at[1 - qi], w_core[wave], pair_sems.at[2 * wave], pair_sems.at[2 * wave + 1], sibling
+        )
+
+    def w_copy(wave, offset):
+        return remote(
+            w_sum[wave].at[lax.bitwise_xor(me, offset)],
+            w_recv[wave].at[offset],
+            w_sems.at[2 * wave],
+            w_sems.at[2 * wave + 1],
+            away(offset),
+        )
+
+    def spread(wave):
+        core_copy(wave).wait_recv()
+        w_sum[wave][...] = (w_part[wave][qi].astype(F32) + w_core[wave][...].astype(F32)).astype(BF16)
+        each(group, lambda i: w_copy(wave, group - i).start())
+
     starts = range(0, cell_count, chunk)
     second_part = jnp.zeros((1, channels), F32)
     down_part = jnp.zeros((hidden_count, channels), F32)
-    gate_part = jnp.zeros((channels, hidden_count), F32)
     for start in starts:
         at = slice(start, start + chunk)
         scaled = post_scaled[at]
         after = post_normed[at]
         second_part += jnp.sum(scaled * after, axis=0, keepdims=True)
         updated_grad = norm_backward(scaled * gain_second, after, inverses[at, 1:2])
-        updated_low = updated_grad.astype(BF16)
         post_scaled[at] = updated_grad
-        down_part += dot(hidden_t[:, at], updated_low, 1, 0)
-        hidden_grad = dot(updated_low, down_ref[...], 1, 1)
+        updated_low[at] = updated_grad.astype(BF16)
+        down_part += dot(hidden_t[:, at], updated_low[at], 1, 0)
+    for t in range(tiles):
+        put(t, down_part[t * channels : (t + 1) * channels])
+    if waves > 1:
+        core_copy(0).start()
+
+    gate_part = jnp.zeros((channels, hidden_count), F32)
+    for start in starts:
+        at = slice(start, start + chunk)
+        hidden_grad = dot(updated_low[at], down_ref[...], 1, 1)
         gate_low = (hidden_grad * gate_coef[at]).astype(BF16)
         up_low[at] = (hidden_grad * up_coef[at]).astype(BF16)
         gate_part += dot(pre_low_t[:, at], gate_low, 1, 0)
         hidden[at] = gate_low
-
     for t in range(tiles):
-        at = slice(t * channels, (t + 1) * channels)
-        put(t, down_part[at])
-        put(tiles + t, gate_part[:, at])
-
-    def core_copy(wave):
-        return remote(
-            w_part[wave].at[1 - qi], w_core[wave], pair_sems.at[2 * wave], pair_sems.at[2 * wave + 1], sibling
-        )
-
+        put(tiles + t, gate_part[:, t * channels : (t + 1) * channels])
     if waves > 1:
-        core_copy(0).start()
-
-    first_part = jnp.zeros((1, channels), F32)
+        core_copy(1).start()
+
     up_part = jnp.zeros((channels, hidden_count), F32)
     for start in starts:
         at = slice(start, start + chunk)
         up_part += dot(pre_low_t[:, at], up_low[at], 1, 0)
+    for t in range(tiles):
+        put(2 * tiles + t, up_part[:, t * channels : (t + 1) * channels])
+    core_copy(waves - 1).start()
+    for wave in range(waves):
+        spread(wave)
+
+    first_part = jnp.zeros((1, channels), F32)
+    for start in starts:
+        at = slice(start, start + chunk)
         pre_scaled = dot(hidden[at], gate_ref[...], 1, 1) + dot(up_low[at], up_ref[...], 1, 1)
         first_part += jnp.sum(pre_scaled * pre_normed[at], axis=0, keepdims=True)
         post_normed[at] = pre_scaled
-    for t in range(tiles):
-        put(2 * tiles + t, up_part[:, t * channels : (t + 1) * channels])
-    core_copy(waves - 1).start()
 
     tail_part[0:HEADS] = head_part.astype(BF16)
     tail_part[HEADS:] = jnp.concatenate(
@@ -490,15 +515,6 @@
     def tail_back(offset):
         return remote(tail_out, tail_out, tail_sems.at[4], tail_sems.at[5], away(offset))
 
-    def w_copy(wave, offset):
-        return remote(
-            w_sum[wave].at[lax.bitwise_xor(me, offset)],
-            w_recv[wave].at[offset],
-            w_sems.at[2 * wave],
-            w_sems.at[2 * wave + 1],
-            away(offset),
-        )
-
     def all_copy(wave, offset):
         at = weight_out[wave].at[qi, me]
         return remote(at, at, all_sems.at[2 * wave], all_sems.at[2 * wave + 1], away(offset))
@@ -510,10 +526,6 @@
     def pair_of(sems, wave):
         return sems.at[pl.ds(2 * wave, 2)]
 
-    for wave in range(waves):
-        core_copy(wave).wait_recv()
-        w_sum[wave][...] = (w_part[wave][qi].astype(F32) + w_core[wave][...].astype(F32)).astype(BF16)
-        each(group, lambda i: w_copy(wave, group - i).start())
     tail_core_copy.wait_recv()
     tail_sum[...] = (tail_part[...].astype(F32) + tail_core[...].astype(F32)).astype(BF16)
 
@@ -673,7 +685,7 @@
     hidden_count = gate_weight.shape[1]
     devices = n_qi * group
     if hidden_count % (BLOCK * devices) == 0:
-        parts_of = (2 * hidden_count, hidden_count)
+        parts_of = (hidden_count, hidden_count, hidden_count)
     else:
         parts_of = (3 * hidden_count,)
     waves = tuple(
@@ -709,6 +721,7 @@
         pltpu.VMEM((count, hidden_count), BF16),
         pltpu.VMEM((hidden_count, count), BF16),
         pltpu.VMEM((count, hidden_count), BF16),
+        pltpu.VMEM((count, channels), BF16),
         pltpu.VMEM((count, channels), F32),
         pltpu.VMEM((count, channels), BF16),
         pltpu.VMEM((count, 128), F32),

time: 34.5 us -> 34 us (0.986)
  Pallas kernels: 33.7 us -> 33.2 us
    pallas_call x1, Pallas kernels: 32.6 us -> 32.1 us  [local(): pl.pallas_call(run, out_shape=(jax.ShapeDtypeStruct((q_half, width), BF16...]
where the time goes in v5:
time: 34 us; the launch traced here: 33.8 us
  Pallas kernels  33.2 us (98%)
  between operations  0.65 us (2%)
    pallas_call x1, Pallas kernels, local(): pl.pallas_call(run, out_shape=(jax.ShapeDtypeStruct((q_half, width), BF16...  32.1 us
    pallas_call x1, Pallas kernels, local(): pl.pallas_call(finish_all, out_shape=tuple((jax.ShapeDtypeStruct(x.shape,...  1.07 us

profile of v5, /device:TPU:0, one launch (start us, length us, event | category | flops | bytes accessed | tf_op | source)
XLA Modules:
  0.0 33.8 jit_solution(13854104805658389655)
XLA Ops:
  0.6 32.1 %block_backward.1 = (bf16[32,768]{1,0:T(8,128)(2,1)S(1)}, bf16[32,768]{1,0:T(8,128)(2,1)S(1)}, bf16[32,768]{1,0:T(8,128)(2,1)S(1)}, bf16[512,128]{1,0:T(8,128)(2...) custom-call(bf16[64,2,32,128]{3,2,1,0:T(8,128)(2,1)} %refs_0_.1, ...), custom_call_target="tpu_custom_call" | custom-call | tf_op jit(solution)/shard_map/block_backward/pallas_call | solution.py:787
  32.8 1.1 %finish_weights.1 = (bf16[32,768]{1,0:T(8,128)(2,1)}, bf16[32,768]{1,0:T(8,128)(2,1)}, bf16[32,768]{1,0:T(8,128)(2,1)}, bf16[512,128]{1,0:T(8,128)(2,1)}, f32[12...) custom-call(bf16[24,128]{1,0:T(8,128)(2,1)S(1)} %get-tuple-element.2, ...), custom_call_target="tpu_custom_call" | custom-call | tf_op jit(solution)/shard_map/finish_weights/pallas_call | solution.py:828

commit v6 on v5

--- a/solution.py
+++ b/solution.py
@@ -450,7 +450,6 @@
 
     starts = range(0, cell_count, chunk)
     second_part = jnp.zeros((1, channels), F32)
-    down_part = jnp.zeros((hidden_count, channels), F32)
     for start in starts:
         at = slice(start, start + chunk)
         scaled = post_scaled[at]
@@ -459,29 +458,25 @@
         updated_grad = norm_backward(scaled * gain_second, after, inverses[at, 1:2])
         post_scaled[at] = updated_grad
         updated_low[at] = updated_grad.astype(BF16)
-        down_part += dot(hidden_t[:, at], updated_low[at], 1, 0)
+    down_part = dot(hidden_t[...], updated_low[...], 1, 0)
     for t in range(tiles):
         put(t, down_part[t * channels : (t + 1) * channels])
     if waves > 1:
         core_copy(0).start()
 
-    gate_part = jnp.zeros((channels, hidden_count), F32)
     for start in starts:
         at = slice(start, start + chunk)
         hidden_grad = dot(updated_low[at], down_ref[...], 1, 1)
         gate_low = (hidden_grad * gate_coef[at]).astype(BF16)
         up_low[at] = (hidden_grad * up_coef[at]).astype(BF16)
-        gate_part += dot(pre_low_t[:, at], gate_low, 1, 0)
         hidden[at] = gate_low
+    gate_part = dot(pre_low_t[...], hidden[...], 1, 0)
     for t in range(tiles):
         put(tiles + t, gate_part[:, t * channels : (t + 1) * channels])
     if waves > 1:
         core_copy(1).start()
 
-    up_part = jnp.zeros((channels, hidden_count), F32)
-    for start in starts:
-        at = slice(start, start + chunk)
-        up_part += dot(pre_low_t[:, at], up_low[at], 1, 0)
+    up_part = dot(pre_low_t[...], up_low[...], 1, 0)
     for t in range(tiles):
         put(2 * tiles + t, up_part[:, t * channels : (t + 1) * channels])
     core_copy(waves - 1).start()

time: 34 us -> 34 us (level)
  no operation moved by 1% of the time
where the time goes in v6:
time: 34 us; the launch traced here: 33.9 us
  Pallas kernels  33.2 us (98%)
  between operations  0.65 us (2%)
    pallas_call x1, Pallas kernels, local(): pl.pallas_call(run, out_shape=(jax.ShapeDtypeStruct((q_half, width), BF16...  32.1 us
    pallas_call x1, Pallas kernels, local(): pl.pallas_call(finish_all, out_shape=tuple((jax.ShapeDtypeStruct(x.shape,...  1.07 us

profile of v6, /device:TPU:0, one launch (start us, length us, event | category | flops | bytes accessed | tf_op | source)
XLA Modules:
  0.0 33.9 jit_solution(5767332343069957623)
XLA Ops:
  0.6 32.1 %block_backward.1 = (bf16[32,768]{1,0:T(8,128)(2,1)S(1)}, bf16[32,768]{1,0:T(8,128)(2,1)S(1)}, bf16[32,768]{1,0:T(8,128)(2,1)S(1)}, bf16[512,128]{1,0:T(8,128)(2...) custom-call(bf16[64,2,32,128]{3,2,1,0:T(8,128)(2,1)} %refs_0_.1, ...), custom_call_target="tpu_custom_call" | custom-call | tf_op jit(solution)/shard_map/block_backward/pallas_call | solution.py:782
  32.8 1.1 %finish_weights.1 = (bf16[32,768]{1,0:T(8,128)(2,1)}, bf16[32,768]{1,0:T(8,128)(2,1)}, bf16[32,768]{1,0:T(8,128)(2,1)}, bf16[512,128]{1,0:T(8,128)(2,1)}, f32[12...) custom-call(bf16[24,128]{1,0:T(8,128)(2,1)S(1)} %get-tuple-element.2, ...), custom_call_target="tpu_custom_call" | custom-call | tf_op jit(solution)/shard_map/finish_weights/pallas_call | solution.py:823
